TPU v7x, 32 devices: a whole 2x2x4 slice. The times are simulated.
32 devices in a mesh: af: 4 (over y, x), col: 2 (over core), ta: 4 (over z).
Axes of the slice: x: 2, y: 2, z: 4, core: 2. Of those that a mesh axis runs over, the one named last changes fastest.
Arguments:
- hidden: bfloat16 [4, 2048, 1536], P('af', 'col'), may hold values from -6 to 6
- lengths: int32 [4], P('af'), may hold values from 256 to 2048, as said below
- norm_gain: bfloat16 [1536], P(('af', 'col')), may hold values from 0.5 to 1.5
- gate_proj: bfloat16 [1536, 3072], P(('af', 'col'), 'ta'), may hold values from -0.15625 to 0.15625
- input_proj: bfloat16 [1536, 3072], P(('af', 'col'), 'ta'), may hold values from -0.15625 to 0.15625
- state_proj: bfloat16 [1536, 256], P(('af', 'col')), may hold values from -0.15625 to 0.15625
- step_proj: bfloat16 [1536, 48], P(('af', 'col'), 'ta'), may hold values from -0.15625 to 0.15625
- conv_input: float32 [4, 3072], P(None, 'ta'), may hold values from -3 to 3
- conv_input_bias: float32 [3072], P('ta'), may hold values from -3 to 3
- conv_state: float32 [4, 256], replicated, may hold values from -3 to 3
- conv_state_bias: float32 [256], replicated, may hold values from -3 to 3
- step_bias: float32 [48], P('ta'), may hold values from -7 to -3
- decay_log: float32 [48], P('ta'), may hold values from -3 to 1
- skip_gain: float32 [48], P('ta'), may hold values from 0.5 to 1.5
- gated_gain: float32 [3072], P('ta'), may hold values from 0.5 to 1.5
- output_proj: bfloat16 [1536, 3072], P(('af', 'col'), 'ta'), may hold values from -0.109375 to 0.109375
- cotangent: bfloat16 [4, 2048, 1536], P('af', 'col'), may hold values from -6 to 6
Outputs:
- block_out: bfloat16 [4, 2048, 1536], P('af', 'col', 'ta')
- hidden_grad: float32 [4, 2048, 1536], P('af', 'col')
- norm_gain_grad: float32 [1536], P(('af', 'col'))
- gate_proj_grad: float32 [1536, 3072], P(('af', 'col'), 'ta')
- input_proj_grad: float32 [1536, 3072], P(('af', 'col'), 'ta')
- state_proj_grad: float32 [1536, 256], P(('af', 'col'))
- step_proj_grad: float32 [1536, 48], P(('af', 'col'), 'ta')
- conv_input_grad: float32 [4, 3072], P(None, 'ta')
- conv_input_bias_grad: float32 [3072], P('ta')
- conv_state_grad: float32 [4, 256], replicated
- conv_state_bias_grad: float32 [256], replicated
- step_bias_grad: float32 [48], P('ta')
- decay_log_grad: float32 [48], P('ta')
- skip_gain_grad: float32 [48], P('ta')
- gated_gain_grad: float32 [3072], P('ta')
- output_proj_grad: float32 [1536, 3072], P(('af', 'col'), 'ta')
Inputs may be any that keep to these rules, and one draw needn't show every extreme that they name: `lengths`: every sequence has 256 or more tokens; in every draw some sequence has exactly 2048.
All inputs are finite; a program needn't handle non-finite values.
Results may differ from a plain program's by a relative error of at most 0.0095.
The roundings to bfloat16 on the way count: a program that leaves them out, or rounds other values in their place, can miss the bound.
Values may be sent and summed in bfloat16 or wider, within the bound.
No kernel may reach another device: no remote copies, remote signals or barrier semaphores. Data moves between devices by JAX's collectives and lax.ppermute only.
A program may use at most 128 MiB of HBM per device.

v0:
```python
import functools

import jax
import jax.numpy as jnp
from jax import lax
from jax.experimental import pallas as pl
from jax.experimental.pallas import tpu as pltpu
from jax.sharding import PartitionSpec as P


EPS = 1e-05
TB = 128
LANES = 128
SLOT = 16
F32 = jnp.float32
BF16 = jnp.bfloat16


def bit_pairs(axis, bit):
    count = lax.axis_size(axis)
    return [(i, i ^ (1 << bit)) for i in range(count)]


def swap_bit(value, axis, bit):
    return lax.ppermute(value, axis, bit_pairs(axis, bit))


def own_bit(axis, bit):
    return (lax.axis_index(axis) >> bit) & 1


def bits_of(axis):
    return lax.axis_size(axis).bit_length() - 1


def shifted_by(value, axis, steps):
    count = lax.axis_size(axis)
    return lax.ppermute(
        value, axis, [(i, i + steps) for i in range(count) if 0 <= i + steps < count]
    )


def pick(value, index, axis):
    return lax.dynamic_index_in_dim(value, index, axis, False)


def spread_bits(block, axis, order):
    bits = bits_of(axis)
    value = block.reshape((1,) * bits + block.shape)
    for bit in order:
        other = swap_bit(value, axis, bit)
        mine = own_bit(axis, bit)
        dim = bits - 1 - bit
        value = jnp.where(
            mine == 0,
            jnp.concatenate([value, other], axis=dim),
            jnp.concatenate([other, value], axis=dim),
        )
    return value


def place_kernel(splits, where_ref, *refs):
    pieces, outs = refs[:10], refs[10:]
    place = where_ref[1]
    half = pieces[3].shape[0]
    now = pl.program_id(0)
    for which in range(2):
        own, x, y, upper, lower = pieces[5 * which : 5 * which + 5]
        slot = place if which == 0 else 1 - place
        for relative, source in enumerate((own, x, y, None)):

            @pl.when(now == relative)
            def _():
                for (start, stop), out in zip(splits, outs):
                    if source is None:
                        out[pl.ds(slot, 1), 0:half, :] = upper[:, start:stop][None]
                        out[pl.ds(slot, 1), half:, :] = lower[:, start:stop][None]
                    else:
                        out[pl.ds(slot, 1)] = source[:, start:stop][None]


def place_rows(mine, other, widths):
    rows, _ = mine[0].shape
    edges = [sum(widths[:k]) for k in range(len(widths) + 1)]
    where = jnp.stack([lax.axis_index("af"), lax.axis_index("col")]).astype(jnp.int32)
    pieces = list(mine) + list(other)
    outs = pl.pallas_call(
        functools.partial(place_kernel, list(zip(edges[:-1], edges[1:]))),
        grid_spec=pltpu.PrefetchScalarGridSpec(
            num_scalar_prefetch=1,
            grid=(4,),
            in_specs=[pl.BlockSpec(piece.shape, lambda i, at: (0, 0)) for piece in pieces],
            out_specs=[
                pl.BlockSpec((2, rows, w), lambda i, at: (at[0] ^ i, 0, 0)) for w in widths
            ],
        ),
        out_shape=[jax.ShapeDtypeStruct((8, rows, w), mine[0].dtype) for w in widths],
        name="place_rows",
    )(where, *pieces)
    return [out.reshape(8 * rows, out.shape[2]) for out in outs]


def gather_rows(local, widths):
    rows, width = local.shape
    half = rows // 2
    if bits_of("af") == 2:
        x = swap_bit(local, "af", 0)
        y = swap_bit(local, "af", 1)
        upper = swap_bit(x[:half], "af", 1)
        lower = swap_bit(y[half:], "af", 0)
        mine = (local, x, y, upper, lower)
        other = [swap_bit(v, "col", 0) for v in mine]
        return place_rows(mine, other, widths)
    order = list(range(bits_of("af")))
    count = lax.axis_size("af")
    first = spread_bits(local[:half], "af", order).reshape(count, half, width)
    second = spread_bits(local[half:], "af", order[::-1]).reshape(count, half, width)
    mine = jnp.concatenate([first, second], axis=1)
    other = swap_bit(mine, "col", 0)
    place = lax.axis_index("col")
    both = jnp.where(place == 0, jnp.stack([mine, other], 1), jnp.stack([other, mine], 1))
    both = both.reshape(count * 2 * rows, width)
    edges = [sum(widths[:k]) for k in range(len(widths) + 1)]
    return [both[:, i:j] for i, j in zip(edges[:-1], edges[1:])]


def gather_vector(local):
    count = lax.axis_size("af") * 2
    place = lax.axis_index("af") * 2 + lax.axis_index("col")
    own = jnp.arange(count)[:, None] == place
    whole = jnp.where(own, local.astype(F32)[None, :], 0.0).reshape(1, -1)
    return sum_over(sum_over(whole, "af"), "col")


def fold_bits(value, axis, order):
    bits = bits_of(axis)
    for bit in order:
        dim = bits - 1 - bit
        mine = own_bit(axis, bit)
        sent = lax.dynamic_slice_in_dim(value, 1 - mine, 1, dim).astype(BF16)
        kept = lax.dynamic_slice_in_dim(value, mine, 1, dim)
        value = kept.astype(F32) + swap_bit(sent, axis, bit).astype(F32)
    return value.reshape(value.shape[bits:])


def scatter_rows(whole):
    count = lax.axis_size("af")
    bits = bits_of("af")
    width = whole.shape[1]
    rows = whole.shape[0] // (2 * count)
    half = rows // 2
    place = lax.axis_index("col")
    blocks = whole.reshape(count, 2, rows, width)
    got = swap_bit(pick(blocks, 1 - place, 1).astype(BF16), "col", 0)
    summed = pick(blocks, place, 1).astype(F32) + got.astype(F32)
    order = list(range(bits))
    lead = (2,) * bits
    first = fold_bits(summed[:, :half].reshape(lead + (half, width)), "af", order)
    second = fold_bits(summed[:, half:].reshape(lead + (half, width)), "af", order[::-1])
    return jnp.concatenate([first, second], axis=0)


def sum_over(value, axis):
    for bit in range(bits_of(axis)):
        value = value + swap_bit(value, axis, bit)
    return value


def chain_sum_step(part, axis, tick, chunks, got, needed=None):
    count = lax.axis_size(axis)
    place = lax.axis_index(axis)
    rows = part.shape[0] // chunks
    sends, pairs = [], []
    for side, step in enumerate((1, -1)):
        rank = place if step == 1 else count - 1 - place
        senders = [i for i in range(count - 1) if 0 <= tick - i < chunks]
        if len(senders) == 1:
            index = tick - senders[0]
        else:
            index = jnp.clip(tick - rank, 0, chunks - 1)
        sent = lax.dynamic_slice_in_dim(part, index * rows, rows, 0)
        if got is not None:
            sent = (sent.astype(F32) + got[side].astype(F32)).astype(BF16)
        sends.append(sent)
        pairs.append(
            [(i, i + 1) if step == 1 else (count - 1 - i, count - 2 - i) for i in senders]
        )
    extra = () if needed is None else (needed,)
    sends = lax.optimization_barrier(tuple(sends) + extra)[:2]
    out = [lax.ppermute(sends[side], axis, pairs[side]) for side in range(2)]
    return lax.optimization_barrier(tuple(out))


def dot(a, b):
    return jnp.dot(a, b, preferred_element_type=F32)


def dot_t(a, b):
    return lax.dot_general(a, b, (((1,), (1,)), ((), ())), preferred_element_type=F32)


def dot_c0(a, b):
    return lax.dot_general(a, b, (((0,), (0,)), ((), ())), preferred_element_type=F32)


def split3(v):
    high = v.astype(BF16).astype(F32)
    rest = v - high
    middle = rest.astype(BF16).astype(F32)
    low = rest - middle
    return (high + pltpu.roll(middle, SLOT, 1) + pltpu.roll(low, 2 * SLOT, 1)).astype(BF16)


def join3(v):
    return v + pltpu.roll(v, LANES - SLOT, 1) + pltpu.roll(v, LANES - 2 * SLOT, 1)


def head_lanes(v, heads):
    lane = lax.broadcasted_iota(jnp.int32, v.shape, 1)
    return jnp.where(lane < heads, v, 0.0)


def tri(upper):
    row = lax.broadcasted_iota(jnp.int32, (TB, TB), 0)
    col = lax.broadcasted_iota(jnp.int32, (TB, TB), 1)
    return (row <= col) if upper else (row >= col)


def rows8(v):
    out = v[0:8]
    for k in range(8, v.shape[0], 8):
        out = out + v[k : k + 8]
    return out


def low_lanes():
    return lax.broadcasted_iota(jnp.int32, (TB, LANES), 1) < 64


def cut_pair(v, low):
    zero = jnp.zeros_like(v)
    return jnp.concatenate([jnp.where(low, v, zero), jnp.where(low, zero, v)], axis=0)


def forward_states_kernel(
    heads, width, pre_ref, halo_ref, taps_ref, head_ref, e3_ref,
    xp_ref, xbc_ref, slope_ref, dt_ref, state_ref, final_ref, decay_ref,
    pad, state, total,
):
    b = pl.program_id(0)
    conv = xp_ref.shape[1]

    @pl.when(b == 0)
    def _():
        pad[0:8, :] = halo_ref[:, 0:conv].astype(BF16).astype(F32)
        state[...] = jnp.zeros_like(state)
        total[...] = jnp.zeros_like(total)

    @pl.when(b > 0)
    def _():
        pad[0:8, :] = pad[TB : TB + 8, :]

    shifted = pre_ref[:, conv : conv + LANES] + head_ref[0:1, :]
    dt = head_lanes(jax.nn.softplus(shifted), heads)
    la = dt * head_ref[1:2, :]
    cum = head_lanes(join3(dot(tri(False).astype(F32).astype(BF16), split3(la))), heads)
    last = cum[TB - 1 : TB, :]
    dt_ref[:, 0:LANES] = dt
    dt_ref[:, LANES : 2 * LANES] = cum
    dt_ref[:, 2 * LANES : 3 * LANES] = jax.nn.sigmoid(shifted)
    weight = split3(head_lanes(jnp.exp(last - cum) * dt, heads))
    row = lax.broadcasted_iota(jnp.int32, (8, LANES), 0)
    edges = jnp.where(row == 0, jnp.exp(total[...]), jnp.exp(jnp.broadcast_to(last, (8, LANES))))
    edges = dot(split3(head_lanes(edges, heads)), e3_ref[...])
    decay_ref[...] = edges
    total[...] = total[...] + last

    for j in range(0, conv, LANES):
        xb = pre_ref[:, j : j + LANES].astype(BF16)
        xp_ref[:, j : j + LANES] = xb
        pad[8 : 8 + TB, j : j + LANES] = xb.astype(F32)
    for j in list(range(width, conv, LANES)) + list(range(0, width, LANES)):
        xa = jnp.broadcast_to(taps_ref[4:5, j : j + LANES], (TB, LANES))
        for k in range(4):
            xa = xa + taps_ref[k : k + 1, j : j + LANES] * pad[5 + k : 5 + k + TB, j : j + LANES]
        sig = jax.nn.sigmoid(xa)
        act = (xa * sig).astype(BF16)
        xbc_ref[:, j : j + LANES] = act
        slope_ref[:, j : j + LANES] = (sig * (1.0 + xa * (1.0 - sig))).astype(BF16)
        if j < width:
            entering = state[:, j : j + LANES]
            state_ref[:, j : j + LANES] = entering
            wx = (dot(weight, e3_ref[:, j : j + LANES]) * act.astype(F32)).astype(BF16)
            fresh = dot_c0(xbc_ref[:, width : width + LANES], wx)
            leaving = edges[1:2, j : j + LANES] * entering + fresh
            state[:, j : j + LANES] = leaving
            final_ref[:, j : j + LANES] = leaving


def forward_states(pre, halo, taps, head, e3, heads, width):
    rows, full = pre.shape
    conv = full - LANES
    blocks = rows // TB
    block = lambda w: pl.BlockSpec((TB, w), lambda b: (b, 0))
    whole = lambda a: pl.BlockSpec(a.shape, lambda b: (0, 0))
    return pl.pallas_call(
        functools.partial(forward_states_kernel, heads, width),
        grid=(blocks,),
        in_specs=[block(full), whole(halo), whole(taps), whole(head), whole(e3)],
        out_specs=[
            block(conv), block(conv), block(conv), block(3 * LANES), block(width),
            pl.BlockSpec((LANES, width), lambda b: (0, 0)),
            pl.BlockSpec((8, width), lambda b: (b, 0)),
        ],
        out_shape=[
            jax.ShapeDtypeStruct((rows, conv), BF16),
            jax.ShapeDtypeStruct((rows, conv), BF16),
            jax.ShapeDtypeStruct((rows, conv), BF16),
            jax.ShapeDtypeStruct((rows, 3 * LANES), F32),
            jax.ShapeDtypeStruct((blocks * LANES, width), F32),
            jax.ShapeDtypeStruct((LANES, width), F32),
            jax.ShapeDtypeStruct((8 * blocks, width), F32),
        ],
        scratch_shapes=[
            pltpu.VMEM((TB + 8, conv), F32),
            pltpu.VMEM((LANES, width), F32),
            pltpu.VMEM((8, LANES), F32),
        ],
        name="forward_states",
    )(pre, halo, taps, head, e3)


def decay_matrix(cum, cum_t, h):
    return jnp.exp(jnp.minimum(cum[:, h : h + 1] - cum_t[h : h + 1, :], 0.0))


def forward_outputs_kernel(
    heads, width, xbc_ref, dt_ref, state_ref, carry_ref, decay_ref, z_ref, dyn_ref,
    chan_ref, e3_ref, y_ref, enter_ref, sums_ref,
):
    write = xbc_ref[:, width : width + LANES]
    read = xbc_ref[:, width + LANES : width + 2 * LANES]
    dt = split3(dt_ref[:, 0:LANES])
    cum = dt_ref[:, LANES : 2 * LANES]
    grown = split3(head_lanes(jnp.exp(cum), heads))
    cum_t = cum.T
    scores = jnp.where(tri(False), dot_t(read, write), 0.0)
    low = low_lanes()
    squares = jnp.zeros((TB, LANES), F32)
    inner = jnp.zeros((TB, LANES), F32)
    for j in range(0, width, LANES):
        h = j // 64
        sl = slice(j, j + LANES)
        x = xbc_ref[:, sl].astype(F32)
        xd = (dot(dt, e3_ref[:, sl]) * x).astype(BF16)
        entering = (state_ref[:, sl] + decay_ref[0:1, sl] * carry_ref[:, sl]).astype(BF16)
        enter_ref[:, sl] = entering
        mix = jnp.concatenate(
            [(scores * decay_matrix(cum, cum_t, h + q)).astype(BF16) for q in range(2)], axis=1
        )
        y = dot(mix, cut_pair(xd, low))
        y = y + dot(grown, e3_ref[:, sl]) * dot(read, entering)
        y = y + chan_ref[0:1, sl] * x
        y_ref[:, sl] = y
        z = z_ref[:, sl]
        gated = y * (z * jax.nn.sigmoid(z))
        squares = squares + gated * gated
        inner = inner + dyn_ref[:, sl] * chan_ref[1:2, sl] * gated
    row = lax.broadcasted_iota(jnp.int32, (8, TB), 0)
    sq = jnp.sum(squares.T, axis=0, keepdims=True)
    dots = jnp.sum(inner.T, axis=0, keepdims=True)
    sums_ref[...] = jnp.where(row == 0, sq, jnp.where(row == 1, dots, 0.0))


def forward_outputs(xbc, dt, state, carry, decay, z, dyn, chan, e3, heads, width):
    rows, conv = xbc.shape
    blocks = rows // TB
    block = lambda w: pl.BlockSpec((TB, w), lambda b: (b, 0))
    whole = lambda a: pl.BlockSpec(a.shape, lambda b: (0, 0))
    return pl.pallas_call(
        functools.partial(forward_outputs_kernel, heads, width),
        grid=(blocks,),
        in_specs=[
            block(conv), block(3 * LANES), block(width), whole(carry),
            pl.BlockSpec((8, width), lambda b: (b, 0)), block(width), block(width),
            whole(chan), whole(e3),
        ],
        out_specs=[block(width), block(width), pl.BlockSpec((8, TB), lambda b: (0, b))],
        out_shape=[
            jax.ShapeDtypeStruct((rows, width), F32),
            jax.ShapeDtypeStruct((blocks * LANES, width), BF16),
            jax.ShapeDtypeStruct((8, rows), F32),
        ],
        name="forward_outputs",
    )(xbc, dt, state, carry, decay, z, dyn, chan, e3)


def backward_states_kernel(
    heads, width, total_inner, xbc_ref, dt_ref, y_ref, z_ref, dyn_ref, sums_ref, chan_ref, e3_ref,
    yn_ref, dssd_ref, dz_ref, gain_ref, dstate_ref, dfinal_ref, decay_ref,
    dstate, total,
):
    i = pl.program_id(0)

    @pl.when(i == 0)
    def _():
        dstate[...] = jnp.zeros_like(dstate)
        total[...] = jnp.zeros_like(total)
        gain_ref[...] = jnp.zeros_like(gain_ref)

    read = xbc_ref[:, width + LANES : width + 2 * LANES]
    cum = dt_ref[:, LANES : 2 * LANES]
    last = cum[TB - 1 : TB, :]
    grown = split3(head_lanes(jnp.exp(cum), heads))
    row = lax.broadcasted_iota(jnp.int32, (8, LANES), 0)
    edges = jnp.where(row == 0, jnp.exp(total[...]), jnp.exp(jnp.broadcast_to(last, (8, LANES))))
    edges = dot(split3(head_lanes(edges, heads)), e3_ref[...])
    decay_ref[...] = edges
    total[...] = total[...] + last
    scale_row = lax.rsqrt(sums_ref[0:1, :] / total_inner + EPS)
    inner_row = sums_ref[1:2, :] / total_inner
    scale = jnp.broadcast_to(scale_row, (TB, TB)).T
    inner = jnp.broadcast_to(scale_row * scale_row * scale_row * inner_row, (TB, TB)).T
    for j in range(0, width, LANES):
        sl = slice(j, j + LANES)
        y = y_ref[:, sl]
        z = z_ref[:, sl]
        dyn = dyn_ref[:, sl]
        gain = chan_ref[1:2, sl]
        sig = jax.nn.sigmoid(z)
        act = z * sig
        gated = y * act
        scaled = gated * scale
        yn_ref[:, sl] = (scaled * gain).astype(BF16)
        gain_ref[:, sl] += rows8(dyn * scaled)
        dgated = scale * (dyn * gain) - gated * inner
        dssd = (dgated * act).astype(BF16)
        dssd_ref[:, sl] = dssd
        slope = sig * (1.0 + z * (1.0 - sig))
        dz_ref[:, sl] = (dgated * y * slope).astype(BF16)
        edy = (dot(grown, e3_ref[:, sl]) * dssd.astype(F32)).astype(BF16)
        leaving = dstate[:, sl]
        dstate_ref[:, sl] = leaving
        entering = edges[1:2, sl] * leaving + dot_c0(read, edy)
        dstate[:, sl] = entering
        dfinal_ref[:, sl] = entering


def backward_states(xbc, dt, y, z, dyn, sums, chan, e3, heads, width, total_inner):
    rows, conv = xbc.shape
    blocks = rows // TB
    back = blocks - 1
    block = lambda w: pl.BlockSpec((TB, w), lambda i: (back - i, 0))
    whole = lambda a: pl.BlockSpec(a.shape, lambda i: (0, 0))
    return pl.pallas_call(
        functools.partial(backward_states_kernel, heads, width, float(total_inner)),
        grid=(blocks,),
        in_specs=[
            block(conv), block(3 * LANES), block(width), block(width), block(width),
            pl.BlockSpec((8, TB), lambda i: (0, back - i)), whole(chan), whole(e3),
        ],
        out_specs=[
            block(width), block(width), block(width),
            pl.BlockSpec((8, width), lambda i: (0, 0)),
            block(width),
            pl.BlockSpec((LANES, width), lambda i: (0, 0)),
            pl.BlockSpec((8, width), lambda i: (back - i, 0)),
        ],
        out_shape=[
            jax.ShapeDtypeStruct((rows, width), BF16),
            jax.ShapeDtypeStruct((rows, width), BF16),
            jax.ShapeDtypeStruct((rows, width), BF16),
            jax.ShapeDtypeStruct((8, width), F32),
            jax.ShapeDtypeStruct((blocks * LANES, width), F32),
            jax.ShapeDtypeStruct((LANES, width), F32),
            jax.ShapeDtypeStruct((8 * blocks, width), F32),
        ],
        scratch_shapes=[pltpu.VMEM((LANES, width), F32), pltpu.VMEM((8, LANES), F32)],
        name="backward_states",
    )(xbc, dt, y, z, dyn, sums, chan, e3)


def backward_inputs_kernel(
    heads, width, reaches_start, xbc_ref, xp_ref, slope_ref, dt_ref, y_ref, dssd_ref, enter_ref,
    dstate_ref, dcarry_ref, decay_ref, next_ref, halo_ref, taps_ref, head_ref, chan_ref, e3_ref,
    dpre_ref, tail_ref, first_ref, rim_ref, conv_ref, headg_ref, skip_ref,
    pad, rim, grown_dy, weighted_x, dleave,
):
    i = pl.program_id(0)
    conv = xp_ref.shape[1]

    @pl.when(i == 0)
    def _():
        pad[TB : TB + 8, :] = next_ref[...]
        conv_ref[...] = jnp.zeros_like(conv_ref)
        headg_ref[...] = jnp.zeros_like(headg_ref)
        skip_ref[...] = jnp.zeros_like(skip_ref)

    @pl.when(i > 0)
    def _():
        pad[TB : TB + 8, :] = pad[0:8, :]

    write = xbc_ref[:, width : width + LANES]
    read = xbc_ref[:, width + LANES : width + 2 * LANES]
    dt_own = dt_ref[:, 0:LANES]
    cum = dt_ref[:, LANES : 2 * LANES]
    last = cum[TB - 1 : TB, :]
    dt = split3(dt_own)
    grown = split3(head_lanes(jnp.exp(cum), heads))
    fading = split3(head_lanes(jnp.exp(last - cum), heads))
    cum_t = cum.T
    causal = tri(False)
    scores = jnp.where(causal, dot_t(read, write), 0.0)
    low = low_lanes()
    dscores = jnp.zeros((TB, TB), F32)
    e1 = e3_ref[0:SLOT, :]
    dcum = jnp.zeros((TB, SLOT), F32)
    ddt = jnp.zeros((TB, SLOT), F32)
    through = jnp.zeros((8, SLOT), F32)

    def head_sum(v, sl):
        high = v.astype(BF16)
        rest = (v - high.astype(F32)).astype(BF16)
        return dot_t(high, e1[:, sl]) + dot_t(rest, e1[:, sl])

    for j in range(0, width, LANES):
        h = j // 64
        sl = slice(j, j + LANES)
        xb = xbc_ref[:, sl]
        x = xb.astype(F32)
        dyb = dssd_ref[:, sl]
        dy = dyb.astype(F32)
        dt_wide = dot(dt, e3_ref[:, sl])
        fading_wide = dot(fading, e3_ref[:, sl])
        xdb = (dt_wide * x).astype(BF16)
        xd = xdb.astype(F32)
        dy_cut = cut_pair(dyb, low)
        dmix = dot_t(dy_cut, xdb)
        mixes = []
        for q in range(2):
            fade = decay_matrix(cum, cum_t, h + q)
            dscores = dscores + dmix[q * TB : (q + 1) * TB] * fade
            mixes.append((scores * fade).astype(BF16))
        dxd = dot_c0(jnp.concatenate(mixes, axis=0), dy_cut)
        leave = dstate_ref[:, sl] + decay_ref[0:1, sl] * dcarry_ref[:, sl]
        leaveb = leave.astype(BF16)
        dleave[:, sl] = leaveb
        tail = fading_wide * dot(write, leaveb)
        dxd = dxd + tail
        skip = chan_ref[0:1, sl]
        dx = dt_wide * dxd + skip * dy
        pad[0:TB, sl] = dx * slope_ref[:, sl].astype(F32)
        grown_dy[:, sl] = (dot(grown, e3_ref[:, sl]) * dy).astype(BF16)
        weighted_x[:, sl] = (fading_wide * dt_wide * x).astype(BF16)
        dcum = dcum + head_sum(dy * (y_ref[:, sl] - skip * x) - xd * dxd, sl)
        ddt = ddt + head_sum(x * dxd, sl)
        enter = enter_ref[:, sl].astype(F32)
        edge = rows8(xd * tail) + rows8(leave * enter) * decay_ref[1:2, sl]
        through = through + head_sum(edge, sl)
        skip_ref[:, sl] += rows8(dy * x)

    dscores = jnp.where(causal, dscores, 0.0).astype(BF16)
    dread = dot(dscores, write) + dot_t(grown_dy[...], enter_ref[...])
    dwrite = dot_c0(dscores, read) + dot_t(weighted_x[...], dleave[...])
    pad[0:TB, width : width + LANES] = dwrite * slope_ref[:, width : width + LANES].astype(F32)
    pad[0:TB, width + LANES : conv] = dread * slope_ref[:, width + LANES : conv].astype(F32)

    blank = jnp.zeros((TB, LANES - SLOT), F32)
    dcum = jnp.concatenate([dcum, blank], axis=1)
    ddt = jnp.concatenate([ddt, blank], axis=1)
    through = jnp.concatenate([jnp.sum(through, axis=0, keepdims=True), blank[0:1]], axis=1)
    dla = join3(dot(tri(True).astype(F32).astype(BF16), split3(dcum)))
    dla = head_lanes(dla + through, heads)
    ddt = ddt + head_ref[1:2, :] * dla
    du = head_lanes(ddt * dt_ref[:, 2 * LANES : 3 * LANES], heads)
    dpre_ref[:, conv : conv + LANES] = du.astype(BF16)
    headg_ref[0:8, :] += rows8(du)
    headg_ref[8:16, :] += rows8(dla * dt_own)

    for j in range(0, conv, LANES):
        sl = slice(j, j + LANES)
        xp = xp_ref[:, sl].astype(F32)
        dxp = jnp.zeros((TB, LANES), F32)
        for k in range(4):
            piece = pad[3 - k : 3 - k + TB, sl]
            dxp = dxp + taps_ref[k : k + 1, sl] * piece
            conv_ref[8 * k : 8 * k + 8, sl] += rows8(xp * piece)
            if k == 3:
                conv_ref[32:40, sl] += rows8(piece)
        dpre_ref[:, sl] = dxp.astype(BF16)

        @pl.when(i == 0)
        def _():
            tail_ref[:, sl] = dxp[TB - 8 : TB]

    @pl.when(i == pl.num_programs(0) - 1)
    def _():
        first_ref[...] = pad[0:8, :]
        rim[0:8, :] = jnp.zeros((8, conv), F32)
        rim[8:16, :] = pad[0:8, :]
        xp = halo_ref[:, 0:conv].astype(BF16).astype(F32)
        out = jnp.zeros((8, conv), F32)
        for k in range(4):
            piece = rim[3 - k : 11 - k, :]
            out = out + taps_ref[k : k + 1, :] * piece
            if reaches_start:
                conv_ref[8 * k : 8 * k + 8, :] += xp * piece
        rim_ref[...] = out


def backward_inputs(
    xbc, xp, slope, dt, y, dssd, enter, dstate, dcarry, decay, after, halo, taps, head, chan, e3,
    heads, width, start, blocks,
):
    conv = xbc.shape[1]
    rows = blocks * TB
    back = start + blocks - 1
    block = lambda w: pl.BlockSpec((TB, w), lambda i: (back - i, 0))
    whole = lambda a: pl.BlockSpec(a.shape, lambda i: (0, 0))
    kept = lambda r, w: pl.BlockSpec((r, w), lambda i: (0, 0))
    return pl.pallas_call(
        functools.partial(backward_inputs_kernel, heads, width, start == 0),
        grid=(blocks,),
        in_specs=[
            block(conv), block(conv), block(conv), block(3 * LANES), block(width), block(width),
            block(width), block(width), whole(dcarry),
            pl.BlockSpec((8, width), lambda i: (back - i, 0)),
            whole(after), whole(halo), whole(taps), whole(head), whole(chan), whole(e3),
        ],
        out_specs=[
            pl.BlockSpec((TB, conv + LANES), lambda i: (blocks - 1 - i, 0)),
            kept(8, conv), kept(8, conv), kept(8, conv), kept(40, conv),
            kept(16, LANES), kept(8, width),
        ],
        out_shape=[
            jax.ShapeDtypeStruct((rows, conv + LANES), BF16),
            jax.ShapeDtypeStruct((8, conv), F32),
            jax.ShapeDtypeStruct((8, conv), F32),
            jax.ShapeDtypeStruct((8, conv), F32),
            jax.ShapeDtypeStruct((40, conv), F32),
            jax.ShapeDtypeStruct((16, LANES), F32),
            jax.ShapeDtypeStruct((8, width), F32),
        ],
        scratch_shapes=[
            pltpu.VMEM((TB + 8, conv), F32),
            pltpu.VMEM((16, conv), F32),
            pltpu.VMEM((TB, width), BF16),
            pltpu.VMEM((TB, width), BF16),
            pltpu.VMEM((LANES, width), BF16),
        ],
        name="backward_inputs",
    )(
        xbc, xp, slope, dt, y, dssd, enter, dstate, dcarry, decay, after, halo, taps, head, chan,
        e3,
    )


def finish_kernel(axis, count, steps, aliased, own_ref, h_ref, cot_ref, gain_ref, *rest):
    arrived, rest = rest[: 2 * (count - 1)], rest[2 * (count - 1) + aliased :]
    out_ref, got, sems = rest
    rows, model = own_ref.shape
    place = lax.axis_index(axis)
    ranks = (place, count - 1 - place)
    now = pl.program_id(0)

    def copy(side, i, step):
        at = pl.ds(step * rows, rows)
        return pltpu.make_async_copy(
            arrived[side * (count - 1) + i - 1].at[at], got.at[side, at], sems.at[side, step]
        )

    @pl.when(now == 0)
    def _():
        for side, rank in enumerate(ranks):
            for i in range(1, count):

                @pl.when(rank == i)
                def _():
                    for step in range(steps):
                        copy(side, i, step).start()

            @pl.when(rank == 0)
            def _():
                got[side] = jnp.zeros((steps * rows, model), BF16)

    for side, rank in enumerate(ranks):
        for i in range(1, count):

            @pl.when(rank == i)
            def _():
                copy(side, i, now).wait()

    gain = gain_ref[0:1, :]
    first = now * rows
    for k in range(0, rows, 16):
        at = pl.ds(k, 16)
        there = pl.ds(pl.multiple_of(first + k, 16), 16)
        hf = h_ref[at, :].astype(F32)
        inverse = lax.rsqrt(jnp.sum(hf * hf, axis=-1, keepdims=True) / model + EPS)
        total = own_ref[at, :].astype(F32) + got[0, there, :].astype(F32)
        weighted = (total + got[1, there, :].astype(F32)) * gain
        inner = jnp.sum(weighted * hf, axis=-1, keepdims=True) / model
        out_ref[at, :] = (
            cot_ref[at, :].astype(F32) + inverse * weighted
            - hf * (inverse * inverse * inverse * inner)
        )


def finish(chunk, chunks, own, h, cot, gain, right, left, so_far):
    rows, model = own.shape[0] // chunks, own.shape[1]
    steps = 4
    piece = rows // steps
    count = len(right) + 1
    anywhere = pl.BlockSpec(memory_space=pl.ANY)
    block = pl.BlockSpec((piece, model), lambda i: (chunk * steps + i, 0))
    operands = [own, h, cot, gain, *right, *left]
    specs = [
        block, block, block,
        pl.BlockSpec(gain.shape, lambda i: (0, 0)),
    ] + [anywhere] * (2 * (count - 1))
    aliases = {}
    if so_far is not None:
        aliases = {len(operands): 0}
        operands.append(so_far)
        specs.append(anywhere)
    return pl.pallas_call(
        functools.partial(finish_kernel, "ta", count, steps, so_far is not None),
        grid=(steps,),
        in_specs=specs,
        out_specs=block,
        out_shape=jax.ShapeDtypeStruct(h.shape, F32),
        scratch_shapes=[pltpu.VMEM((2, rows, model), BF16), pltpu.SemaphoreType.DMA((2, steps))],
        input_output_aliases=aliases,
        name="finish",
    )(*operands)


def outer(left, right):
    return lax.dot_general(left, right, (((0,), (0,)), ((), ())), preferred_element_type=F32)


def against(left, right):
    return lax.dot_general(left, right, (((1,), (1,)), ((), ())), preferred_element_type=F32)


def product(left, right):
    return jnp.dot(left, right, preferred_element_type=F32)


def row_of(values, width):
    return jnp.pad(values.astype(F32), (0, width - values.shape[0]))[None, :]


def program(
    hidden, lengths, norm_gain, gate_proj, input_proj, state_proj, step_proj, conv_input,
    conv_input_bias, conv_state, conv_state_bias, step_bias, decay_log, skip_gain, gated_gain,
    output_proj, cotangent,
):
    _, positions, model = hidden.shape
    heads = step_bias.shape[0]
    width = gated_gain.shape[0]
    both = state_proj.shape[1]
    conv = width + both
    local_rows = norm_gain.shape[0]
    total_inner = width * lax.axis_size("ta")
    h = hidden[0]
    cot = cotangent[0]

    packed = jnp.concatenate(
        [
            input_proj, state_proj, step_proj,
            jnp.zeros((local_rows, LANES - heads), BF16),
        ],
        axis=1,
    )
    halo_h = shifted_by(h[positions - 8 :], "col", 1)
    (packed_full,) = gather_rows(packed, [packed.shape[1]])
    gate_full = lax.all_gather(gate_proj, ("af", "col"), axis=0, tiled=True)
    output_full = lax.all_gather(output_proj, ("af", "col"), axis=0, tiled=True)
    gain = gather_vector(norm_gain)

    e3 = (
        (jnp.arange(LANES)[:, None] % SLOT == jnp.arange(width)[None, :] // (width // heads))
        & (jnp.arange(LANES)[:, None] < 3 * SLOT)
    ).astype(BF16)
    taps = jnp.concatenate(
        [
            jnp.concatenate([conv_input, conv_state], axis=1),
            jnp.concatenate([conv_input_bias, conv_state_bias])[None, :],
            jnp.zeros((3, conv), F32),
        ],
        axis=0,
    )
    rate = -jnp.exp(decay_log)
    head = jnp.concatenate(
        [row_of(step_bias, LANES), row_of(rate, LANES), jnp.zeros((6, LANES), F32)], axis=0
    )
    chan = jnp.concatenate(
        [
            jnp.repeat(skip_gain, width // heads)[None, :], gated_gain[None, :],
            jnp.zeros((6, width), F32),
        ],
        axis=0,
    )

    def normalise(rows):
        values = rows.astype(F32)
        inverse = lax.rsqrt(jnp.mean(values * values, axis=-1, keepdims=True) + EPS)
        return lax.optimization_barrier((values * inverse * gain).astype(BF16))

    normed = normalise(h)
    halo_normed = normalise(halo_h)
    pre = product(normed, packed_full)
    halo = product(halo_normed, packed_full)
    xp, xbc, slope, dt, state, final, decay = forward_states(
        pre, halo, taps, head, e3, heads, width
    )
    carry = shifted_by(final, "col", 1)
    z = product(normed, gate_full)

    position = lax.axis_index("col") * positions + jnp.arange(positions)
    valid = (position < lengths[0]).astype(F32)[:, None]
    dmix = (cot.astype(F32) * valid).astype(BF16)
    dyn = product(dmix, output_full)
    y, enter, sums = forward_outputs(xbc, dt, state, carry, decay, z, dyn, chan, e3, heads, width)
    sums = sum_over(sums, "ta")
    yn, dssd, dz, gain_part, dstate, dfinal, fade = backward_states(
        xbc, dt, y, z, dyn, sums, chan, e3, heads, width, total_inner
    )
    dcarry = shifted_by(dfinal, "col", -1)

    mixed = against(output_full, yn).astype(BF16)
    mixed = lax.psum_scatter(mixed, "ta", scatter_dimension=0, tiled=True)
    quarter = mixed.shape[0]
    own = lax.dynamic_slice_in_dim(h, lax.axis_index("ta") * quarter, quarter, 1).astype(F32)
    block_out = (own + mixed.T.astype(F32) * valid).astype(BF16)

    dpre, tail, _, rim, conv_part, head_part, skip_part = backward_inputs(
        xbc, xp, slope, dt, y, dssd, enter, dstate, dcarry, fade, jnp.zeros((8, conv), F32),
        halo, taps, head, chan, e3, heads, width, 0, positions // TB,
    )
    tail = (tail + shifted_by(rim, "col", -1)).astype(BF16)
    dpre = lax.dynamic_update_slice(dpre, tail, (positions - 8, 0))
    partial = (against(dz, gate_full) + against(dpre, packed_full)).astype(BF16)

    chunks = 4
    count = lax.axis_size("ta")
    gain_rows = jnp.broadcast_to(gain, (8, model))
    hidden_grad, arrived = None, []
    for tick in range(chunks + count - 2):
        arrived.append(
            chain_sum_step(
                partial, "ta", tick, chunks, arrived[-1] if arrived else None,
                mixed if tick == 1 else None,
            )
        )
        at = tick - count + 2
        if at >= 0:
            came = arrived[at : at + count - 1]
            hidden_grad = finish(
                at, chunks, partial, h, cot, gain_rows, [v[0] for v in came],
                [v[1] for v in came], hidden_grad,
            )

    def scattered(value):
        return lax.psum_scatter(
            value.astype(BF16), ("af", "col"), scatter_dimension=0, tiled=True
        ).astype(F32)

    output_grad = outer(dmix, yn)
    gate_grad = outer(normed, dz)
    output_grad = scattered(output_grad)
    gate_grad = scattered(gate_grad)
    packed_grad = outer(normed, dpre).astype(BF16)
    packed_grad = scatter_rows(packed_grad)

    input_grad = packed_grad[:, :width]
    state_grad = packed_grad[:, width:conv]
    step_grad = packed_grad[:, conv : conv + heads]
    rows_dot = (
        jnp.sum(gate_grad * gate_proj.astype(F32), axis=1)
        + jnp.sum(input_grad * input_proj.astype(F32), axis=1)
        + jnp.sum(state_grad * state_proj.astype(F32), axis=1)
        + jnp.sum(step_grad * step_proj.astype(F32), axis=1)
    )

    conv_sums = jnp.sum(conv_part.reshape(5, 8, conv), axis=1)
    head_sums = jnp.sum(head_part.reshape(2, 8, LANES), axis=1)
    small = jnp.concatenate(
        [
            jnp.pad(conv_sums, ((0, 0), (0, LANES * 2))),
            jnp.concatenate(
                [
                    jnp.sum(gain_part, axis=0), jnp.zeros((both,), F32), head_sums[0], head_sums[1],
                ]
            )[None, :],
            jnp.pad(jnp.sum(skip_part, axis=0), (0, both + 2 * LANES))[None, :],
            jnp.zeros((1, conv + 2 * LANES), F32),
        ],
        axis=0,
    )
    small = sum_over(sum_over(small, "col"), "af")
    third = jnp.concatenate(
        [state_grad, jnp.broadcast_to(rows_dot[:, None], (local_rows, LANES))], axis=1
    )
    third = jnp.concatenate([third, jnp.pad(small[:, width:conv], ((0, 0), (0, LANES)))], axis=0)
    third = sum_over(third, "ta")
    state_grad = third[:local_rows, :both]
    norm_gain_grad = third[:local_rows, both] / norm_gain.astype(F32)
    state_small = third[local_rows:, :both]
    skip_grad = jnp.sum(small[6, :width].reshape(heads, width // heads), axis=1)
    return (
        block_out[None],
        hidden_grad[None],
        norm_gain_grad,
        gate_grad,
        input_grad,
        state_grad,
        step_grad,
        small[0:4, :width],
        small[4, :width],
        state_small[0:4],
        state_small[4],
        small[5, conv : conv + heads],
        rate * small[5, conv + LANES : conv + LANES + heads],
        skip_grad,
        small[5, :width],
        output_grad,
    )


def solution(mesh):
    return mapped(mesh)


def mapped(mesh):
    return jax.shard_map(
        program,
        mesh=mesh,
        in_specs=(
            P("af", "col", None),
            P("af"),
            P(("af", "col")),
            P(("af", "col"), "ta"),
            P(("af", "col"), "ta"),
            P(("af", "col"), None),
            P(("af", "col"), "ta"),
            P(None, "ta"),
            P("ta"),
            P(),
            P(),
            P("ta"),
            P("ta"),
            P("ta"),
            P("ta"),
            P(("af", "col"), "ta"),
            P("af", "col", None),
        ),
        out_specs=(
            P("af", "col", "ta"),
            P("af", "col", None),
            P(("af", "col")),
            P(("af", "col"), "ta"),
            P(("af", "col"), "ta"),
            P(("af", "col"), None),
            P(("af", "col"), "ta"),
            P(None, "ta"),
            P("ta"),
            P(),
            P(),
            P("ta"),
            P("ta"),
            P("ta"),
            P("ta"),
            P(("af", "col"), "ta"),
        ),
        check_vma=False,
    )
```

profile of v0, /device:TPU:10, one launch (start us, length us, event | category | flops | bytes accessed | tf_op | source)
XLA Modules:
  0.0 385.6 jit_solution(9959141203974901689)
XLA Ops:
  38.5 7.1 %collective-permute-done.5.refs_3_ = bf16[96,1152]{1,0:T(8,128)(2,1)S(1)} collective-permute-done((bf16[96,1152]{1,0:T(8,128)(2,1)S(1)}, bf16[96,1152]{1,0:T(8,128)(2,1)S(1)}, u32[]{:S(2)}, u32[]{:S(2)}) %collective-permute-start.5) | collective-permute-done | bytes 221216 | tf_op jit(solution)/shard_map/ppermute | solution.py:25
  48.8 5.3 %place_rows.1 = bf16[8,192,1152]{2,1,0:T(8,128)(2,1)} custom-call(s32[2]{0:T(128)} %pad_add_fusion.where_ref, bf16[192,1152]{1,0:T(8,128)(2,1)} %concatenate.33.refs_0_, bf16[192,1152]{1,0:T(8,128)(2,1)} %collective-permute-done.3.refs_1_, bf16[192,1152]{1,0:T(8,128)(2,1)} %collective-permute-done.4.refs_2_, bf16[96,1152]{1,0:T(8,128)(2,1)} %copy-done.21, ...), custom_call_target="tpu_custom_call" | custom-call | tf_op jit(solution)/shard_map/place_rows/pallas_call | solution.py:87
  57.6 5.9 %fusion.26.pre_ref = f32[1024,1152]{1,0:T(8,128)} fusion(bf16[1024,1536]{1,0:T(8,128)(2,1)S(1)} %copy-done.11, bf16[1536,1152]{1,0:T(8,128)(2,1)S(1)} %bitcast.93), kind=kOutput, calls=%fused_computation.104 | convolution fusion | flops 3623878656 | bytes 11403264 | tf_op jit(solution)/shard_map/dot_general | solution.py:747
  63.5 13.9 %forward_states.1 = (bf16[1024,1024]{1,0:T(8,128)(2,1)}, bf16[1024,1024]{1,0:T(8,128)(2,1)}, bf16[1024,1024]{1,0:T(8,128)(2,1)}, f32[1024,384]{1,0:T(8,128)}, f3...) custom-call(f32[1024,1152]{1,0:T(8,128)} %fusion.26.pre_ref, f32[8,1152]{1,0:T(8,128)} %fusion.27.halo_ref, ...), custom_call_target="tpu_custom_call" | custom-call | tf_op jit(solution)/shard_map/forward_states/pallas_call | solution.py:306
  80.1 6.1 %fusion.7.dyn_ref = f32[1024,768]{1,0:T(8,128)} fusion(bf16[1536,768]{1,0:T(8,128)(2,1)} %all-gather.5.cloned.1.call-done, f32[1024]{0:T(1024)S(1)} %fusion.18, bf16[1,1024,1536]{2,1,0:T(8,128)(2,1)S(1)} %copy-done.2), kind=kOutput, calls=%fused_computation.28 | convolution fusion | flops 2420637696 | bytes 8654848 | tf_op jit(solution)/shard_map/dot_general | solution.py:747
  86.1 6.9 %fusion.28.z_ref = f32[1024,768]{1,0:T(8,128)} fusion(bf16[1024,1536]{1,0:T(8,128)(2,1)} %fusion.2, bf16[1536,768]{1,0:T(8,128)(2,1)} %all-gather.3.cloned.1.call-done), kind=kOutput, calls=%fused_computation.106 | convolution fusion | flops 2415919104 | bytes 8650752 | tf_op jit(solution)/shard_map/dot_general | solution.py:747
  93.7 11.9 %forward_outputs.1 = (f32[1024,768]{1,0:T(8,128)}, bf16[1024,768]{1,0:T(8,128)(2,1)}, f32[8,1024]{1,0:T(8,128)}) custom-call(bf16[1024,1024]{1,0:T(8,128)(2,1)} %get-tuple-element.63.xbc_ref, f32[1024,384]{1,0:T(8,128)} %get-tuple-element.64.dt_ref, f32[1024,768]{1,0:T(8,128)} %get-tuple-element.65.state_ref, f32[128,768]{1,0:T(8,128)} %copy-done.18, ...), custom_call_target="tpu_custom_call" | custom-call | tf_op jit(solution)/shard_map/forward_outputs/pallas_call | solution.py:380
  116.0 11.9 %backward_states.1 = (bf16[1024,768]{1,0:T(8,128)(2,1)}, bf16[1024,768]{1,0:T(8,128)(2,1)}, bf16[1024,768]{1,0:T(8,128)(2,1)}, f32[8,768]{1,0:T(8,128)}, f32[102...) custom-call(bf16[1024,1024]{1,0:T(8,128)(2,1)} %get-tuple-element.63.xbc_ref, ...), custom_call_target="tpu_custom_call" | custom-call | tf_op jit(solution)/shard_map/backward_states/pallas_call | solution.py:455
  138.6 5.4 %convolution_convert_fusion.3 = bf16[1536,768]{1,0:T(8,128)(2,1)} fusion(bf16[1024,1536]{1,0:T(8,128)(2,1)S(1)} %copy-done.12, bf16[1024,768]{1,0:T(8,128)(2,1)} %get-tuple-element.71), kind=kOutput, calls=%fused_computation.11 | convolution fusion | flops 2417098752 | bytes 7077888 | tf_op jit(solution)/shard_map/dot_general | solution.py:739
  144.2 7.5 %fusion.29 = f32[1024,1536]{1,0:T(8,128)} fusion(bf16[1024,768]{1,0:T(8,128)(2,1)} %get-tuple-element.71, bf16[1536,768]{1,0:T(8,128)(2,1)} %all-gather.3.cloned.1.call-done), kind=kOutput, calls=%fused_computation.107 | convolution fusion | flops 2415919104 | bytes 10223616 | tf_op jit(solution)/shard_map/dot_general | solution.py:743
  152.5 27.4 %backward_inputs.1 = (bf16[1024,1152]{1,0:T(8,128)(2,1)}, f32[8,1024]{1,0:T(8,128)}, f32[8,1024]{1,0:T(8,128)}, f32[8,1024]{1,0:T(8,128)}, f32[40,1024]{1,0:T(8,...) custom-call(bf16[1024,1024]{1,0:T(8,128)(2,1)} %get-tuple-element.63.xbc_ref, bf16[1024,1024]{1,0:T(8,128)(2,1)} %get-tuple-element.72.xp_ref, ...), custom_call_target="tpu_custom_call" | custom-call | tf_op jit(solution)/shard_map/backward_inputs/pallas_call | solution.py:621
  187.0 6.4 %convolution_convert_fusion = bf16[1536,1152]{1,0:T(8,128)(2,1)S(1)} fusion(bf16[1024,1536]{1,0:T(8,128)(2,1)S(1)} %copy-done.12, bf16[1024,1152]{1,0:T(8,128)(2,1)} %fusion.15), kind=kOutput, calls=%fused_computation.2 | convolution fusion | flops 3625648128 | bytes 9043968 | tf_op jit(solution)/shard_map/dot_general | solution.py:739
  210.6 6.8 %convolution_convert_fusion.2 = bf16[1536,768]{1,0:T(8,128)(2,1)} fusion(bf16[1024,768]{1,0:T(8,128)(2,1)} %get-tuple-element.70, f32[1024]{0:T(1024)S(1)} %fusion.18, bf16[1,1024,1536]{2,1,0:T(8,128)(2,1)} %param.33), kind=kOutput, calls=%fused_computation.10 | convolution fusion | flops 2421817344 | bytes 7081984 | tf_op jit(solution)/shard_map/dot_general | solution.py:739
  218.1 6.4 %collective-permute-done.18.rest_0_ = bf16[256,1536]{1,0:T(8,128)(2,1)} collective-permute-done((bf16[256,1536]{1,0:T(8,128)(2,1)}, bf16[256,1536]{1,0:T(8,128)(2,1)}, u32[]{:S(2)}, u32[]{:S(2)}) %collective-permute-start.18) | collective-permute-done | bytes 786464 | tf_op jit(solution)/shard_map/ppermute | solution.py:190
  232.7 7.6 %collective-permute-done.31 = bf16[2,1,96,1152]{3,2,1,0:T(8,128)(2,1)S(1)} collective-permute-done((bf16[2,1,96,1152]{3,2,1,0:T(8,128)(2,1)S(1)}, bf16[2,1,96,1152]{3,2,1,0:T(8,128)(2,1)S(1)}, u32[]{:S(2)}, u32[]{:S(2)}) %collective-permute-start.31) | collective-permute-done | bytes 442400 | tf_op jit(solution)/shard_map/ppermute | solution.py:25
  243.6 6.3 %collective-permute-start.20 = (bf16[256,1536]{1,0:T(8,128)(2,1)}, bf16[256,1536]{1,0:T(8,128)(2,1)S(1)}, u32[]{:S(2)}, u32[]{:S(2)}) collective-permute-start(bf16[256,1536]{1,0:T(8,128)(2,1)} %get-tuple-element.86), channel_id=1, source_target_pairs={{0,1},{1,2},{4,5},{5,6},{8,9},{9,10},{12,13},{13,14},{16,17},{17,1... | collective-permute-start | bytes 2359304 | tf_op jit(solution)/shard_map/ppermute | solution.py:190
  255.4 7.8 %collective-permute-done.20.rest_1_.rest_0_ = bf16[256,1536]{1,0:T(8,128)(2,1)S(1)} collective-permute-done((bf16[256,1536]{1,0:T(8,128)(2,1)}, bf16[256,1536]{1,0:T(8,128)(2,1)S(1)}, u32[]{:S(2)}, u32[]{:S(2)}) %collective-permute-start.20) | collective-permute-done | bytes 786464 | tf_op jit(solution)/shard_map/ppermute | solution.py:190
  274.2 10.1 %collective-permute-done.22.rest_2_.rest_1_.rest_0_ = bf16[256,1536]{1,0:T(8,128)(2,1)S(1)} collective-permute-done((bf16[256,1536]{1,0:T(8,128)(2,1)S(1)}, bf16[256,1536]{1,0:T(8,128)(2,1)S(1)}, u32[]{:S(2)}, u32[]{:S(2)}) %collective-permute-start.22) | collective-permute-done | bytes 786464 | tf_op jit(solution)/shard_map/ppermute | solution.py:190
  320.7 10.6 %collective-permute-done.38 = f32[200,384]{1,0:T(8,128)} collective-permute-done((f32[200,384]{1,0:T(8,128)}, f32[200,384]{1,0:T(8,128)}, u32[]{:S(2)}, u32[]{:S(2)}) %collective-permute-start.38) | collective-permute-done | bytes 307232 | tf_op jit(solution)/shard_map/ppermute | solution.py:25
  337.6 6.8 %collective-permute-start.29 = (bf16[256,1536]{1,0:T(8,128)(2,1)}, bf16[256,1536]{1,0:T(8,128)(2,1)S(1)}, u32[]{:S(2)}, u32[]{:S(2)}) collective-permute-start(bf16[256,1536]{1,0:T(8,128)(2,1)} %get-tuple-element.103), channel_id=1, source_target_pairs={{1,0},{5,4},{9,8},{13,12},{17,16},{21,20},{25,24},{29,28}} | collective-permute-start | bytes 2359304 | tf_op jit(solution)/shard_map/ppermute | solution.py:190
  354.9 5.5 %finish.4.rest_6_ = f32[1024,1536]{1,0:T(8,128)} custom-call(bf16[1024,1536]{1,0:T(8,128)(2,1)} %copy-done, bf16[1024,1536]{1,0:T(8,128)(2,1)} %bitcast.83, bf16[1024,1536]{1,0:T(8,128)(2,1)} %bitcast.88, f32[8,1536]{1,0:T(8,128)} %mul.118.gain_ref, bf16[256,1536]{1,0:T(8,128)(2,1)} %collective-permute-done.18.rest_0_, bf16[256,1536]{1,0:T(8,128)(2,1)} %copy-done.7, ...), custom_call_target="tpu_custom_call" | custom-call | tf_op jit(solution)/shard_map/finish/pallas_call | solution.py:726
  360.5 5.5 %finish.5.rest_6_ = f32[1024,1536]{1,0:T(8,128)} custom-call(bf16[1024,1536]{1,0:T(8,128)(2,1)} %copy-done, bf16[1024,1536]{1,0:T(8,128)(2,1)} %bitcast.84, bf16[1024,1536]{1,0:T(8,128)(2,1)} %bitcast.89, f32[8,1536]{1,0:T(8,128)} %mul.118.gain_ref, bf16[256,1536]{1,0:T(8,128)(2,1)} %copy-done.7, ...), custom_call_target="tpu_custom_call", output_to_operand_aliasing={{}: (10, {})} | custom-call | tf_op jit(solution)/shard_map/finish/pallas_call | solution.py:726
  366.0 5.5 %finish.6.rest_6_ = f32[1024,1536]{1,0:T(8,128)} custom-call(bf16[1024,1536]{1,0:T(8,128)(2,1)} %copy-done, bf16[1024,1536]{1,0:T(8,128)(2,1)} %bitcast.85, bf16[1024,1536]{1,0:T(8,128)(2,1)} %bitcast.90, f32[8,1536]{1,0:T(8,128)} %mul.118.gain_ref, bf16[256,1536]{1,0:T(8,128)(2,1)} %copy-done.5, ...), custom_call_target="tpu_custom_call", output_to_operand_aliasing={{}: (10, {})} | custom-call | tf_op jit(solution)/shard_map/finish/pallas_call | solution.py:726
  373.3 5.5 %finish.7 = f32[1024,1536]{1,0:T(8,128)} custom-call(bf16[1024,1536]{1,0:T(8,128)(2,1)} %copy-done, bf16[1024,1536]{1,0:T(8,128)(2,1)} %bitcast.86, bf16[1024,1536]{1,0:T(8,128)(2,1)} %bitcast.91, f32[8,1536]{1,0:T(8,128)} %mul.118.gain_ref, bf16[256,1536]{1,0:T(8,128)(2,1)} %collective-permute-done.24.rest_2_.rest_1_.rest_0_, ...), custom_call_target="tpu_custom_call", output_to_operand_aliasing={{}: (10, {})} | custom-call | tf_op jit(solution)/shard_map/finish/pallas_call | solution.py:726
  (278 shorter events, 169.9 us)
Async XLA Ops:
  7.2 72.9 %all-gather.5.cloned.1.call-start = ((), (), s32[]{:S(2)}) async-start(), calls=%async_computation.4 | async-start | bytes 2654208 | tf_op jit(solution)/shard_map/all_gather | solution.py:779
  8.0 78.1 %all-gather.3.cloned.1.call-start = ((), (), s32[]{:S(2)}) async-start(), calls=%async_computation.3 | async-start | bytes 2654208 | tf_op jit(solution)/shard_map/all_gather | solution.py:778
  10.9 23.1 %collective-permute-start.3 = (bf16[192,1152]{1,0:T(8,128)(2,1)}, bf16[192,1152]{1,0:T(8,128)(2,1)}, u32[]{:S(2)}, u32[]{:S(2)}) collective-permute-start(bf16[192,1152]{1,0:T(8,128)(2,1)} %concatenate.33.refs_0_), channel_id=1, source_target_pairs={{0,8},{8,0},{16,24},{24,16},{1,9},{9,1},{17,25},{25,17},{2,10},{10... | collective-permute-start | bytes 1327112 | tf_op jit(solution)/shard_map/ppermute | solution.py:25
  11.4 25.1 %collective-permute-start.4 = (bf16[192,1152]{1,0:T(8,128)(2,1)}, bf16[192,1152]{1,0:T(8,128)(2,1)}, u32[]{:S(2)}, u32[]{:S(2)}) collective-permute-start(bf16[192,1152]{1,0:T(8,128)(2,1)} %concatenate.33.refs_0_), channel_id=1, source_target_pairs={{0,16},{8,24},{16,0},{24,8},{1,17},{9,25},{17,1},{25,9},{2,18},{10... | collective-permute-start | bytes 1327112 | tf_op jit(solution)/shard_map/ppermute | solution.py:25
  12.9 33.2 %collective-permute-start.7 = (bf16[192,1152]{1,0:T(8,128)(2,1)}, bf16[192,1152]{1,0:T(8,128)(2,1)}, u32[]{:S(2)}, u32[]{:S(2)}) collective-permute-start(bf16[192,1152]{1,0:T(8,128)(2,1)} %concatenate.33.refs_0_), channel_id=1, source_target_pairs={{0,4},{4,0},{1,5},{5,1},{2,6},{6,2},{3,7},{7,3},{8,12},{12,8},{9,1... | collective-permute-start | bytes 1327112 | tf_op jit(solution)/shard_map/ppermute | solution.py:25
  16.0 17.8 %collective-permute-start.12 = (bf16[8,1536]{1,0:T(8,128)(2,1)S(1)}, bf16[8,1536]{1,0:T(8,128)(2,1)S(1)}, u32[]{:S(2)}, u32[]{:S(2)}) collective-permute-start(bf16[8,1536]{1,0:T(8,128)(2,1)S(1)} %slice_bitcast_fusion), channel_id=1, source_target_pairs={{0,4},{1,5},{2,6},{3,7},{8,12},{9,13},{10,14},{11,15},{16,20},{17,... | collective-permute-start | bytes 73736 | tf_op jit(solution)/shard_map/ppermute | solution.py:38
  18.2 223.2 %reduce-scatter.10.cloned.1.call-start = ((), (), s32[]{:S(2)}) async-start(), calls=%async_computation.7 | async-start | bytes 3932160
  135.8 161.1 %reduce-scatter.6.cloned.1.call-start = ((), (), s32[]{:S(2)}) async-start(), calls=%async_computation.5 | async-start | bytes 2654208 | tf_op jit(solution)/shard_map/reduce_scatter | solution.py:866
  144.0 202.3 %reduce-scatter.8.cloned.1.call-start = ((), (), s32[]{:S(2)}) async-start(), calls=%async_computation.6 | async-start | bytes 2654208 | tf_op jit(solution)/shard_map/reduce_scatter | solution.py:866
  184.4 21.5 %collective-permute-start.35 = (f32[8,1280]{1,0:T(8,128)S(1)}, f32[8,1280]{1,0:T(8,128)S(1)}, u32[]{:S(2)}, u32[]{:S(2)}) collective-permute-start(f32[8,1280]{1,0:T(8,128)S(1)} %fusion.14), channel_id=1, source_target_pairs={{0,4},{4,0},{1,5},{5,1},{2,6},{6,2},{3,7},{7,3},{8,12},{12,8},{9,1... | collective-permute-start | bytes 122888 | tf_op jit(solution)/shard_map/ppermute | solution.py:25
  196.1 28.4 %collective-permute-start.30 = (bf16[4,192,1152]{2,1,0:T(8,128)(2,1)}, bf16[4,192,1152]{2,1,0:T(8,128)(2,1)}, u32[]{:S(2)}, u32[]{:S(2)}) collective-permute-start(bf16[4,192,1152]{2,1,0:T(8,128)(2,1)} %dynamic-slice_bitcast_fusion), channel_id=1, source_target_pairs={{0,4},{4,0},{1,5},{5,1},{2,6},{6,2},{3,7},{7,3},{8,12},{12,8},{9,1... | collective-permute-start | bytes 5308424 | tf_op jit(solution)/shard_map/ppermute | solution.py:25
  202.9 21.6 %collective-permute-start.18 = (bf16[256,1536]{1,0:T(8,128)(2,1)}, bf16[256,1536]{1,0:T(8,128)(2,1)}, u32[]{:S(2)}, u32[]{:S(2)}) collective-permute-start(bf16[256,1536]{1,0:T(8,128)(2,1)} %dynamic_slice.87), channel_id=1, source_target_pairs={{0,1},{4,5},{8,9},{12,13},{16,17},{20,21},{24,25},{28,29}} | collective-permute-start | bytes 2359304 | tf_op jit(solution)/shard_map/ppermute | solution.py:190
  204.1 20.3 %collective-permute-start.19 = (bf16[256,1536]{1,0:T(8,128)(2,1)}, bf16[256,1536]{1,0:T(8,128)(2,1)}, u32[]{:S(2)}, u32[]{:S(2)}) collective-permute-start(bf16[256,1536]{1,0:T(8,128)(2,1)} %dynamic_slice.87), channel_id=1, source_target_pairs={{3,2},{7,6},{11,10},{15,14},{19,18},{23,22},{27,26},{31,30}} | collective-permute-start | bytes 2359304 | tf_op jit(solution)/shard_map/ppermute | solution.py:190
  231.6 21.4 %collective-permute-start.33 = (bf16[1,2,96,1152]{3,2,1,0:T(8,128)(2,1)}, bf16[1,2,96,1152]{3,2,1,0:T(8,128)(2,1)}, u32[]{:S(2)}, u32[]{:S(2)}) collective-permute-start(bf16[1,2,96,1152]{3,2,1,0:T(8,128)(2,1)} %dynamic-slice_convert_fusion), channel_id=1, source_target_pairs={{0,16},{8,24},{16,0},{24,8},{1,17},{9,25},{17,1},{25,9},{2,18},{10... | collective-permute-start | bytes 1327112 | tf_op jit(solution)/shard_map/ppermute | solution.py:25
  243.6 19.6 %collective-permute-start.20 = (bf16[256,1536]{1,0:T(8,128)(2,1)}, bf16[256,1536]{1,0:T(8,128)(2,1)S(1)}, u32[]{:S(2)}, u32[]{:S(2)}) collective-permute-start(bf16[256,1536]{1,0:T(8,128)(2,1)} %get-tuple-element.86), channel_id=1, source_target_pairs={{0,1},{1,2},{4,5},{5,6},{8,9},{9,10},{12,13},{13,14},{16,17},{17,1... | collective-permute-start | bytes 2359304 | tf_op jit(solution)/shard_map/ppermute | solution.py:190
  249.9 17.3 %collective-permute-start.21 = (bf16[256,1536]{1,0:T(8,128)(2,1)}, bf16[256,1536]{1,0:T(8,128)(2,1)S(1)}, u32[]{:S(2)}, u32[]{:S(2)}) collective-permute-start(bf16[256,1536]{1,0:T(8,128)(2,1)} %get-tuple-element.87), channel_id=1, source_target_pairs={{3,2},{2,1},{7,6},{6,5},{11,10},{10,9},{15,14},{14,13},{19,18},{18... | collective-permute-start | bytes 2359304 | tf_op jit(solution)/shard_map/ppermute | solution.py:190
  252.3 21.7 %collective-permute-start.32 = (bf16[1,1,96,1152]{3,2,1,0:T(8,128)(2,1)S(1)}, bf16[1,1,96,1152]{3,2,1,0:T(8,128)(2,1)S(1)}, u32[]{:S(2)}, u32[]{:S(2)}) collective-permute-start(bf16[1,1,96,1152]{3,2,1,0:T(8,128)(2,1)S(1)} %dynamic-slice_convert_fusion.3), channel_id=1, source_target_pairs={{0,16},{8,24},{16,0},{24,8},{1,17},{9,25},{17,1},{25,9},{2,18},{10... | collective-permute-start | bytes 663560 | tf_op jit(solution)/shard_map/ppermute | solution.py:25
  254.4 19.8 %collective-permute-start.34 = (bf16[1,1,96,1152]{3,2,1,0:T(8,128)(2,1)S(1)}, bf16[1,1,96,1152]{3,2,1,0:T(8,128)(2,1)S(1)}, u32[]{:S(2)}, u32[]{:S(2)}) collective-permute-start(bf16[1,1,96,1152]{3,2,1,0:T(8,128)(2,1)S(1)} %dynamic-slice_convert_fusion.2), channel_id=1, source_target_pairs={{0,8},{8,0},{16,24},{24,16},{1,9},{9,1},{17,25},{25,17},{2,10},{10... | collective-permute-start | bytes 663560 | tf_op jit(solution)/shard_map/ppermute | solution.py:25
  268.1 16.2 %collective-permute-start.22 = (bf16[256,1536]{1,0:T(8,128)(2,1)S(1)}, bf16[256,1536]{1,0:T(8,128)(2,1)S(1)}, u32[]{:S(2)}, u32[]{:S(2)}) collective-permute-start(bf16[256,1536]{1,0:T(8,128)(2,1)S(1)} %get-tuple-element.90), channel_id=1, source_target_pairs={{0,1},{1,2},{2,3},{4,5},{5,6},{6,7},{8,9},{9,10},{10,11},{12,13},{... | collective-permute-start | bytes 2359304 | tf_op jit(solution)/shard_map/ppermute | solution.py:190
  270.1 16.2 %collective-permute-start.23 = (bf16[256,1536]{1,0:T(8,128)(2,1)S(1)}, bf16[256,1536]{1,0:T(8,128)(2,1)S(1)}, u32[]{:S(2)}, u32[]{:S(2)}) collective-permute-start(bf16[256,1536]{1,0:T(8,128)(2,1)S(1)} %get-tuple-element.91), channel_id=1, source_target_pairs={{3,2},{2,1},{1,0},{7,6},{6,5},{5,4},{11,10},{10,9},{9,8},{15,14},{... | collective-permute-start | bytes 2359304 | tf_op jit(solution)/shard_map/ppermute | solution.py:190
  308.6 25.4 %collective-permute-start.26 = (bf16[256,1536]{1,0:T(8,128)(2,1)}, bf16[256,1536]{1,0:T(8,128)(2,1)}, u32[]{:S(2)}, u32[]{:S(2)}) collective-permute-start(bf16[256,1536]{1,0:T(8,128)(2,1)} %get-tuple-element.98), channel_id=1, source_target_pairs={{1,2},{2,3},{5,6},{6,7},{9,10},{10,11},{13,14},{14,15},{17,18},{18... | collective-permute-start | bytes 2359304 | tf_op jit(solution)/shard_map/ppermute | solution.py:190
  311.5 22.4 %collective-permute-start.27 = (bf16[256,1536]{1,0:T(8,128)(2,1)}, bf16[256,1536]{1,0:T(8,128)(2,1)}, u32[]{:S(2)}, u32[]{:S(2)}) collective-permute-start(bf16[256,1536]{1,0:T(8,128)(2,1)} %get-tuple-element.99), channel_id=1, source_target_pairs={{2,1},{1,0},{6,5},{5,4},{10,9},{9,8},{14,13},{13,12},{18,17},{17,1... | collective-permute-start | bytes 2359304 | tf_op jit(solution)/shard_map/ppermute | solution.py:190
  336.9 34.6 %collective-permute-start.28 = (bf16[256,1536]{1,0:T(8,128)(2,1)}, bf16[256,1536]{1,0:T(8,128)(2,1)S(1)}, u32[]{:S(2)}, u32[]{:S(2)}) collective-permute-start(bf16[256,1536]{1,0:T(8,128)(2,1)} %get-tuple-element.102), channel_id=1, source_target_pairs={{2,3},{6,7},{10,11},{14,15},{18,19},{22,23},{26,27},{30,31}} | collective-permute-start | bytes 2359304 | tf_op jit(solution)/shard_map/ppermute | solution.py:190
  337.6 33.9 %collective-permute-start.29 = (bf16[256,1536]{1,0:T(8,128)(2,1)}, bf16[256,1536]{1,0:T(8,128)(2,1)S(1)}, u32[]{:S(2)}, u32[]{:S(2)}) collective-permute-start(bf16[256,1536]{1,0:T(8,128)(2,1)} %get-tuple-element.103), channel_id=1, source_target_pairs={{1,0},{5,4},{9,8},{13,12},{17,16},{21,20},{25,24},{29,28}} | collective-permute-start | bytes 2359304 | tf_op jit(solution)/shard_map/ppermute | solution.py:190
  (64 other events, 879.0 us)
Sparse Core Ops, SparseCore 0:
  9.9 35.5 all-gather.4
  47.4 28.7 all-gather.2
  135.9 60.1 reduce-scatter.9
  199.2 46.3 reduce-scatter.5
  249.3 42.3 reduce-scatter.7
where the time goes:
time: 393 us; the launch traced here: 386 us
  Pallas kernels  92.5 us (24%)
  waiting for transfers between devices  77.8 us (20%)
  starting transfers between devices  62.4 us (16%)
  matrix products  57.7 us (15%)
  other arithmetic  47.3 us (12%)
  local copies, waits for them, and re-layouts  32.3 us (8%)
  between operations  15.5 us (4%)
    ppermute x24, waiting for transfers between devices, swap_bit(): return lax.ppermute(value, axis, bit_pairs(axis, bit))  40 us
    ppermute x12, waiting for transfers between devices, chain_sum_step(): out = [lax.ppermute(sends[side], axis, pairs[side]) for side in range(2)]  37.1 us
    ppermute x12, starting transfers between devices, chain_sum_step(): out = [lax.ppermute(sends[side], axis, pairs[side]) for side in range(2)]  36.6 us
    pallas_call x1, Pallas kernels, backward_inputs(): pl.pallas_call(functools.partial(backward_inputs_kernel, heads, width, st...  27.4 us
    dot_general x4, matrix products, product(): return jnp.dot(left, right, preferred_element_type=F32)  22.3 us
    pallas_call x4, Pallas kernels, finish(): pl.pallas_call(functools.partial(finish_kernel, 'ta', count, steps, so_fa...  22 us
    dot_general x3, matrix products, outer(): lax.dot_general(left, right, (((0,), (0,)), ((), ())), preferred_element_...  18.7 us
    ppermute x24, starting transfers between devices, swap_bit(): return lax.ppermute(value, axis, bit_pairs(axis, bit))  18 us
  transfers between devices with their start and end apart: 45, of which 18 were waited for; matrix products, arithmetic and copies ran while one was open for 31% of the time, Pallas kernels for 16%

commit v1 on v0

--- a/solution.py
+++ b/solution.py
@@ -12,6 +12,7 @@
 TB = 128
 LANES = 128
 SLOT = 16
+GRANT = 52 * 1024 * 1024
 F32 = jnp.float32
 BF16 = jnp.bfloat16
 
@@ -96,6 +97,7 @@
         ),
         out_shape=[jax.ShapeDtypeStruct((8, rows, w), mine[0].dtype) for w in widths],
         name="place_rows",
+        compiler_params=pltpu.CompilerParams(vmem_limit_bytes=GRANT),
     )(where, *pieces)
     return [out.reshape(8 * rows, out.shape[2]) for out in outs]
 
@@ -130,6 +132,10 @@
     own = jnp.arange(count)[:, None] == place
     whole = jnp.where(own, local.astype(F32)[None, :], 0.0).reshape(1, -1)
     return sum_over(sum_over(whole, "af"), "col")
+
+
+def after(value, *others):
+    return lax.optimization_barrier((value,) + others)[0]
 
 
 def fold_bits(value, axis, order):
@@ -327,6 +333,7 @@
             pltpu.VMEM((8, LANES), F32),
         ],
         name="forward_states",
+        compiler_params=pltpu.CompilerParams(vmem_limit_bytes=GRANT),
     )(pre, halo, taps, head, e3)
 
 
@@ -392,6 +399,7 @@
             jax.ShapeDtypeStruct((8, rows), F32),
         ],
         name="forward_outputs",
+        compiler_params=pltpu.CompilerParams(vmem_limit_bytes=GRANT),
     )(xbc, dt, state, carry, decay, z, dyn, chan, e3)
 
 
@@ -477,6 +485,7 @@
         ],
         scratch_shapes=[pltpu.VMEM((LANES, width), F32), pltpu.VMEM((8, LANES), F32)],
         name="backward_states",
+        compiler_params=pltpu.CompilerParams(vmem_limit_bytes=GRANT),
     )(xbc, dt, y, z, dyn, sums, chan, e3)
 
 
@@ -649,6 +658,7 @@
             pltpu.VMEM((LANES, width), BF16),
         ],
         name="backward_inputs",
+        compiler_params=pltpu.CompilerParams(vmem_limit_bytes=GRANT),
     )(
         xbc, xp, slope, dt, y, dssd, enter, dstate, dcarry, decay, after, halo, taps, head, chan,
         e3,
@@ -708,7 +718,7 @@
 
 def finish(chunk, chunks, own, h, cot, gain, right, left, so_far):
     rows, model = own.shape[0] // chunks, own.shape[1]
-    steps = 4
+    steps = 2
     piece = rows // steps
     count = len(right) + 1
     anywhere = pl.BlockSpec(memory_space=pl.ANY)
@@ -732,6 +742,7 @@
         scratch_shapes=[pltpu.VMEM((2, rows, model), BF16), pltpu.SemaphoreType.DMA((2, steps))],
         input_output_aliases=aliases,
         name="finish",
+        compiler_params=pltpu.CompilerParams(vmem_limit_bytes=GRANT),
     )(*operands)
 
 
@@ -869,8 +880,8 @@
 
     output_grad = outer(dmix, yn)
     gate_grad = outer(normed, dz)
-    output_grad = scattered(output_grad)
-    gate_grad = scattered(gate_grad)
+    gate_grad = scattered(after(gate_grad.astype(BF16), mixed))
+    output_grad = scattered(after(output_grad.astype(BF16), gate_grad))
     packed_grad = outer(normed, dpre).astype(BF16)
     packed_grad = scatter_rows(packed_grad)
 
@@ -900,14 +911,19 @@
         axis=0,
     )
     small = sum_over(sum_over(small, "col"), "af")
+    gains = jnp.pad(rows_dot, (0, -local_rows % both)).reshape(-1, both)
     third = jnp.concatenate(
-        [state_grad, jnp.broadcast_to(rows_dot[:, None], (local_rows, LANES))], axis=1
-    )
-    third = jnp.concatenate([third, jnp.pad(small[:, width:conv], ((0, 0), (0, LANES)))], axis=0)
+        [
+            state_grad, small[:, width:conv], gains,
+            jnp.zeros((-gains.shape[0] % 8, both), F32),
+        ],
+        axis=0,
+    )
     third = sum_over(third, "ta")
-    state_grad = third[:local_rows, :both]
-    norm_gain_grad = third[:local_rows, both] / norm_gain.astype(F32)
-    state_small = third[local_rows:, :both]
+    state_grad = third[:local_rows]
+    state_small = third[local_rows:]
+    gains = third[local_rows + 8 : local_rows + 8 + gains.shape[0]].reshape(-1)
+    norm_gain_grad = gains[:local_rows] / norm_gain.astype(F32)
     skip_grad = jnp.sum(small[6, :width].reshape(heads, width // heads), axis=1)
     return (
         block_out[None],

time: 393 us -> 389 us (0.990)
  the two profiles are of different devices: /device:TPU:10 before, /device:TPU:18 now
where the time goes in v1:
time: 389 us; the launch traced here: 382 us
  waiting for transfers between devices  98.2 us (25%)
  Pallas kernels  86.1 us (22%)
  starting transfers between devices  59.6 us (15%)
  matrix products  56.2 us (14%)
  other arithmetic  35.4 us (9%)
  local copies, waits for them, and re-layouts  30.6 us (8%)
  between operations  15.7 us (4%)
    ppermute x12, waiting for transfers between devices, chain_sum_step(): out = [lax.ppermute(sends[side], axis, pairs[side]) for side in range(2)]  60.3 us
    ppermute x24, waiting for transfers between devices, swap_bit(): return lax.ppermute(value, axis, bit_pairs(axis, bit))  36.6 us
    ppermute x12, starting transfers between devices, chain_sum_step(): out = [lax.ppermute(sends[side], axis, pairs[side]) for side in range(2)]  30.3 us
    pallas_call x1, Pallas kernels, backward_inputs(): pl.pallas_call(functools.partial(backward_inputs_kernel, heads, width, st...  26.5 us
    dot_general x4, matrix products, product(): return jnp.dot(left, right, preferred_element_type=F32)  22.3 us
    ppermute x24, starting transfers between devices, swap_bit(): return lax.ppermute(value, axis, bit_pairs(axis, bit))  21.6 us
    pallas_call x4, Pallas kernels, finish(): pl.pallas_call(functools.partial(finish_kernel, 'ta', count, steps, so_fa...  18 us
    dot_general x3, matrix products, against(): lax.dot_general(left, right, (((1,), (1,)), ((), ())), preferred_element_...  17.2 us
  transfers between devices with their start and end apart: 45, of which 19 were waited for; matrix products, arithmetic and copies ran while one was open for 25% of the time, Pallas kernels for 16%

profile of v1, /device:TPU:18, one launch (start us, length us, event | category | flops | bytes accessed | tf_op | source)
XLA Modules:
  0.0 381.7 jit_solution(13976108190704025020)
XLA Ops:
  35.3 9.7 %collective-permute-done.5.refs_3_ = bf16[96,1152]{1,0:T(8,128)(2,1)S(1)} collective-permute-done((bf16[96,1152]{1,0:T(8,128)(2,1)S(1)}, bf16[96,1152]{1,0:T(8,128)(2,1)S(1)}, u32[]{:S(2)}, u32[]{:S(2)}) %collective-permute-start.5) | collective-permute-done | bytes 221216 | tf_op jit(solution)/shard_map/ppermute | solution.py:26
  55.9 5.8 %fusion.26.pre_ref = f32[1024,1152]{1,0:T(8,128)} fusion(bf16[1024,1536]{1,0:T(8,128)(2,1)S(1)} %fusion.2, bf16[1536,1152]{1,0:T(8,128)(2,1)S(1)} %bitcast.95), kind=kOutput, calls=%fused_computation.102 | convolution fusion | flops 3623878656 | bytes 11403264 | tf_op jit(solution)/shard_map/dot_general | solution.py:758
  61.7 13.6 %forward_states.1 = (bf16[1024,1024]{1,0:T(8,128)(2,1)}, bf16[1024,1024]{1,0:T(8,128)(2,1)}, bf16[1024,1024]{1,0:T(8,128)(2,1)}, f32[1024,384]{1,0:T(8,128)}, f3...) custom-call(f32[1024,1152]{1,0:T(8,128)} %fusion.26.pre_ref, f32[8,1152]{1,0:T(8,128)S(1)} %fusion.27.halo_ref, ...), custom_call_target="tpu_custom_call" | custom-call | tf_op jit(solution)/shard_map/forward_states/pallas_call | solution.py:312
  77.8 6.9 %fusion.7.dyn_ref = f32[1024,768]{1,0:T(8,128)} fusion(bf16[1536,768]{1,0:T(8,128)(2,1)} %all-gather.5.cloned.1.call-done, f32[1024]{0:T(1024)S(1)} %fusion.18, bf16[1,1024,1536]{2,1,0:T(8,128)(2,1)} %param.33), kind=kOutput, calls=%fused_computation.28 | convolution fusion | flops 2420637696 | bytes 8654848 | tf_op jit(solution)/shard_map/dot_general | solution.py:758
  84.8 6.9 %fusion.28.z_ref = f32[1024,768]{1,0:T(8,128)} fusion(bf16[1024,1536]{1,0:T(8,128)(2,1)} %copy-done.21, bf16[1536,768]{1,0:T(8,128)(2,1)} %all-gather.3.cloned.1.call-done), kind=kOutput, calls=%fused_computation.104 | convolution fusion | flops 2415919104 | bytes 8650752 | tf_op jit(solution)/shard_map/dot_general | solution.py:758
  91.7 11.9 %forward_outputs.1 = (f32[1024,768]{1,0:T(8,128)}, bf16[1024,768]{1,0:T(8,128)(2,1)}, f32[8,1024]{1,0:T(8,128)S(1)}) custom-call(bf16[1024,1024]{1,0:T(8,128)(2,1)} %get-tuple-element.65.xbc_ref, f32[1024,384]{1,0:T(8,128)} %get-tuple-element.66.dt_ref, f32[1024,768]{1,0:T(8,128)} %get-tuple-element.67.state_ref, ...), custom_call_target="tpu_custom_call" | custom-call | tf_op jit(solution)/shard_map/forward_outputs/pallas_call | solution.py:387
  112.3 11.8 %backward_states.1 = (bf16[1024,768]{1,0:T(8,128)(2,1)}, bf16[1024,768]{1,0:T(8,128)(2,1)}, bf16[1024,768]{1,0:T(8,128)(2,1)}, f32[8,768]{1,0:T(8,128)S(1)}, f32...) custom-call(bf16[1024,1024]{1,0:T(8,128)(2,1)} %get-tuple-element.65.xbc_ref, ...), custom_call_target="tpu_custom_call" | custom-call | tf_op jit(solution)/shard_map/backward_states/pallas_call | solution.py:463
  124.2 5.7 %convolution_convert_fusion.2 = bf16[1536,768]{1,0:T(8,128)(2,1)} fusion(bf16[1024,768]{1,0:T(8,128)(2,1)} %get-tuple-element.72, f32[1024]{0:T(1024)S(1)} %fusion.18, bf16[1,1024,1536]{2,1,0:T(8,128)(2,1)S(1)} %copy-done.8), kind=kOutput, calls=%fused_computation.10 | convolution fusion | flops 2421817344 | bytes 7081984 | tf_op jit(solution)/shard_map/dot_general | solution.py:750
  129.8 6.4 %fusion.3 = bf16[1536,1024]{0,1:T(8,128)(2,1)} fusion(bf16[1024,768]{1,0:T(8,128)(2,1)} %get-tuple-element.72, bf16[1536,768]{1,0:T(8,128)(2,1)} %all-gather.5.cloned.1.call-done), kind=kOutput, calls=%fused_computation.12 | convolution fusion | flops 2417491968 | bytes 7077888 | tf_op jit(solution)/shard_map/dot_general | solution.py:754
  136.3 4.6 %copy.42 = bf16[1536,1024]{1,0:T(8,128)(2,1)} copy(bf16[1536,1024]{0,1:T(8,128)(2,1)} %fusion.3) | data formatting | bytes 6291456
  142.6 6.2 %fusion.29 = f32[1024,1536]{1,0:T(8,128)} fusion(bf16[1024,768]{1,0:T(8,128)(2,1)S(1)} %copy-done.47, bf16[1536,768]{1,0:T(8,128)(2,1)} %all-gather.3.cloned.1.call-done), kind=kOutput, calls=%fused_computation.105 | convolution fusion | flops 2415919104 | bytes 10223616 | tf_op jit(solution)/shard_map/dot_general | solution.py:754
  148.8 26.5 %backward_inputs.1 = (bf16[1024,1152]{1,0:T(8,128)(2,1)}, f32[8,1024]{1,0:T(8,128)S(1)}, f32[8,1024]{1,0:T(8,128)}, f32[8,1024]{1,0:T(8,128)S(1)}, f32[40,1024]{...) custom-call(bf16[1024,1024]{1,0:T(8,128)(2,1)} %get-tuple-element.65.xbc_ref, ...), custom_call_target="tpu_custom_call" | custom-call | tf_op jit(solution)/shard_map/backward_inputs/pallas_call | solution.py:630
  179.2 7.0 %convolution_convert_fusion = bf16[1536,1152]{1,0:T(8,128)(2,1)S(1)} fusion(bf16[1024,1536]{1,0:T(8,128)(2,1)} %copy-done.21, bf16[1024,1152]{1,0:T(8,128)(2,1)} %fusion.15), kind=kOutput, calls=%fused_computation.2 | convolution fusion | flops 3625648128 | bytes 9043968 | tf_op jit(solution)/shard_map/dot_general | solution.py:750
  190.2 4.5 %add_convert_fusion.own_ref = bf16[1024,1536]{1,0:T(8,128)(2,1)S(1)} fusion(f32[1024,1536]{1,0:T(8,128)S(1)} %copy-done.51, bf16[1024,1152]{1,0:T(8,128)(2,1)S(1)} %copy-done.46, bf16[1536,1152]{1,0:T(8,128)(2,1)S(1)} %bitcast.96), kind=kOutput, calls=%fused_computation.6 | convolution fusion | flops 3627024384 | bytes 15335424 | tf_op jit(solution)/shard_map/dot_general | solution.py:754
  207.8 11.9 %collective-permute-done.19.rest_3_ = bf16[256,1536]{1,0:T(8,128)(2,1)S(1)} collective-permute-done((bf16[256,1536]{1,0:T(8,128)(2,1)}, bf16[256,1536]{1,0:T(8,128)(2,1)S(1)}, u32[]{:S(2)}, u32[]{:S(2)}) %collective-permute-start.19) | collective-permute-done | bytes 786464 | tf_op jit(solution)/shard_map/ppermute | solution.py:196
  228.7 4.5 %collective-permute-start.21 = (bf16[256,1536]{1,0:T(8,128)(2,1)}, bf16[256,1536]{1,0:T(8,128)(2,1)S(1)}, u32[]{:S(2)}, u32[]{:S(2)}) collective-permute-start(bf16[256,1536]{1,0:T(8,128)(2,1)} %get-tuple-element.89), channel_id=1, source_target_pairs={{3,2},{2,1},{7,6},{6,5},{11,10},{10,9},{15,14},{14,13},{19,18},{18... | collective-permute-start | bytes 2359304 | tf_op jit(solution)/shard_map/ppermute | solution.py:196
  239.2 9.0 %collective-permute-done.20.rest_1_.rest_0_ = bf16[256,1536]{1,0:T(8,128)(2,1)S(1)} collective-permute-done((bf16[256,1536]{1,0:T(8,128)(2,1)}, bf16[256,1536]{1,0:T(8,128)(2,1)S(1)}, u32[]{:S(2)}, u32[]{:S(2)}) %collective-permute-start.20) | collective-permute-done | bytes 786464 | tf_op jit(solution)/shard_map/ppermute | solution.py:196
  260.5 11.6 %collective-permute-done.22.rest_2_.rest_1_.rest_0_ = bf16[256,1536]{1,0:T(8,128)(2,1)S(1)} collective-permute-done((bf16[256,1536]{1,0:T(8,128)(2,1)S(1)}, bf16[256,1536]{1,0:T(8,128)(2,1)S(1)}, u32[]{:S(2)}, u32[]{:S(2)}) %collective-permute-start.22) | collective-permute-done | bytes 786464 | tf_op jit(solution)/shard_map/ppermute | solution.py:196
  282.3 11.5 %collective-permute-done.24.rest_2_.rest_1_.rest_0_ = bf16[256,1536]{1,0:T(8,128)(2,1)S(1)} collective-permute-done((bf16[256,1536]{1,0:T(8,128)(2,1)S(1)}, bf16[256,1536]{1,0:T(8,128)(2,1)S(1)}, u32[]{:S(2)}, u32[]{:S(2)}) %collective-permute-start.24) | collective-permute-done | bytes 786464 | tf_op jit(solution)/shard_map/ppermute | solution.py:196
  308.6 10.1 %collective-permute-done.26.rest_2_.rest_1_ = bf16[256,1536]{1,0:T(8,128)(2,1)S(1)} collective-permute-done((bf16[256,1536]{1,0:T(8,128)(2,1)S(1)}, bf16[256,1536]{1,0:T(8,128)(2,1)S(1)}, u32[]{:S(2)}, u32[]{:S(2)}) %collective-permute-start.26) | collective-permute-done | bytes 786464 | tf_op jit(solution)/shard_map/ppermute | solution.py:196
  329.4 13.0 %collective-permute-done.38 = f32[208,256]{1,0:T(8,128)} collective-permute-done((f32[208,256]{1,0:T(8,128)}, f32[208,256]{1,0:T(8,128)}, u32[]{:S(2)}, u32[]{:S(2)}) %collective-permute-start.38) | collective-permute-done | bytes 213024 | tf_op jit(solution)/shard_map/ppermute | solution.py:26
  343.4 6.6 %collective-permute-start.39 = (f32[208,256]{1,0:T(8,128)S(1)}, f32[208,256]{1,0:T(8,128)S(1)}, u32[]{:S(2)}, u32[]{:S(2)}) collective-permute-start(f32[208,256]{1,0:T(8,128)S(1)} %fusion.23), channel_id=1, source_target_pairs={{0,2},{1,3},{2,0},{3,1},{4,6},{5,7},{6,4},{7,5},{8,10},{9,11},{10,... | collective-permute-start | bytes 638984 | tf_op jit(solution)/shard_map/ppermute | solution.py:26
  357.1 4.5 %finish.5.rest_6_ = f32[1024,1536]{1,0:T(8,128)} custom-call(bf16[1024,1536]{1,0:T(8,128)(2,1)} %copy-done.6, bf16[1024,1536]{1,0:T(8,128)(2,1)} %bitcast.86, bf16[1024,1536]{1,0:T(8,128)(2,1)} %bitcast.91, f32[8,1536]{1,0:T(8,128)S(1)} %mul.118.gain_ref, ...), custom_call_target="tpu_custom_call", output_to_operand_aliasing={{}: (10, {})} | custom-call | tf_op jit(solution)/shard_map/finish/pallas_call | solution.py:736
  361.6 4.5 %finish.6.rest_6_ = f32[1024,1536]{1,0:T(8,128)} custom-call(bf16[1024,1536]{1,0:T(8,128)(2,1)} %copy-done.6, bf16[1024,1536]{1,0:T(8,128)(2,1)} %bitcast.87, bf16[1024,1536]{1,0:T(8,128)(2,1)} %bitcast.92, f32[8,1536]{1,0:T(8,128)S(1)} %mul.118.gain_ref, bf16[256,1536]{1,0:T(8,128)(2,1)S(1)} %copy-done.1, ...), custom_call_target="tpu_custom_call", output_to_operand_aliasing={{}: (10, {})} | custom-call | tf_op jit(solution)/shard_map/finish/pallas_call | solution.py:736
  (298 shorter events, 151.1 us)
Async XLA Ops:
  7.2 70.7 %all-gather.5.cloned.1.call-start = ((), (), s32[]{:S(2)}) async-start(), calls=%async_computation.4 | async-start | bytes 2654208 | tf_op jit(solution)/shard_map/all_gather | solution.py:790
  8.0 76.8 %all-gather.3.cloned.1.call-start = ((), (), s32[]{:S(2)}) async-start(), calls=%async_computation.3 | async-start | bytes 2654208 | tf_op jit(solution)/shard_map/all_gather | solution.py:789
  10.0 23.0 %collective-permute-start.3 = (bf16[192,1152]{1,0:T(8,128)(2,1)S(1)}, bf16[192,1152]{1,0:T(8,128)(2,1)S(1)}, u32[]{:S(2)}, u32[]{:S(2)}) collective-permute-start(bf16[192,1152]{1,0:T(8,128)(2,1)S(1)} %concatenate.30.refs_0_), channel_id=1, source_target_pairs={{0,8},{8,0},{16,24},{24,16},{1,9},{9,1},{17,25},{25,17},{2,10},{10... | collective-permute-start | bytes 1327112 | tf_op jit(solution)/shard_map/ppermute | solution.py:26
  10.6 24.0 %collective-permute-start.4 = (bf16[192,1152]{1,0:T(8,128)(2,1)S(1)}, bf16[192,1152]{1,0:T(8,128)(2,1)S(1)}, u32[]{:S(2)}, u32[]{:S(2)}) collective-permute-start(bf16[192,1152]{1,0:T(8,128)(2,1)S(1)} %concatenate.30.refs_0_), channel_id=1, source_target_pairs={{0,16},{8,24},{16,0},{24,8},{1,17},{9,25},{17,1},{25,9},{2,18},{10... | collective-permute-start | bytes 1327112 | tf_op jit(solution)/shard_map/ppermute | solution.py:26
  12.1 33.5 %collective-permute-start.7 = (bf16[192,1152]{1,0:T(8,128)(2,1)S(1)}, bf16[192,1152]{1,0:T(8,128)(2,1)S(1)}, u32[]{:S(2)}, u32[]{:S(2)}) collective-permute-start(bf16[192,1152]{1,0:T(8,128)(2,1)S(1)} %concatenate.30.refs_0_), channel_id=1, source_target_pairs={{0,4},{4,0},{1,5},{5,1},{2,6},{6,2},{3,7},{7,3},{8,12},{12,8},{9,1... | collective-permute-start | bytes 1327112 | tf_op jit(solution)/shard_map/ppermute | solution.py:26
  17.3 207.8 %reduce-scatter.10.cloned.1.call-start = ((), (), s32[]{:S(2)}) async-start(), calls=%async_computation.7 | async-start | bytes 3932160
  140.9 154.8 %reduce-scatter.6.cloned.1.call-start = ((), (), s32[]{:S(2)}) async-start(), calls=%async_computation.5 | async-start | bytes 2654208 | tf_op jit(solution)/shard_map/reduce_scatter | solution.py:877
  187.6 35.3 %collective-permute-start.30 = (bf16[4,192,1152]{2,1,0:T(8,128)(2,1)}, bf16[4,192,1152]{2,1,0:T(8,128)(2,1)S(1)}, u32[]{:S(2)}, u32[]{:S(2)}) collective-permute-start(bf16[4,192,1152]{2,1,0:T(8,128)(2,1)} %dynamic-slice_bitcast_fusion), channel_id=1, source_target_pairs={{0,4},{4,0},{1,5},{5,1},{2,6},{6,2},{3,7},{7,3},{8,12},{12,8},{9,1... | collective-permute-start | bytes 5308424 | tf_op jit(solution)/shard_map/ppermute | solution.py:26
  198.0 21.7 %collective-permute-start.19 = (bf16[256,1536]{1,0:T(8,128)(2,1)}, bf16[256,1536]{1,0:T(8,128)(2,1)S(1)}, u32[]{:S(2)}, u32[]{:S(2)}) collective-permute-start(bf16[256,1536]{1,0:T(8,128)(2,1)} %dynamic_slice.87), channel_id=1, source_target_pairs={{3,2},{7,6},{11,10},{15,14},{19,18},{23,22},{27,26},{31,30}} | collective-permute-start | bytes 2359304 | tf_op jit(solution)/shard_map/ppermute | solution.py:196
  227.4 20.9 %collective-permute-start.20 = (bf16[256,1536]{1,0:T(8,128)(2,1)}, bf16[256,1536]{1,0:T(8,128)(2,1)S(1)}, u32[]{:S(2)}, u32[]{:S(2)}) collective-permute-start(bf16[256,1536]{1,0:T(8,128)(2,1)} %get-tuple-element.88), channel_id=1, source_target_pairs={{0,1},{1,2},{4,5},{5,6},{8,9},{9,10},{12,13},{13,14},{16,17},{17,1... | collective-permute-start | bytes 2359304 | tf_op jit(solution)/shard_map/ppermute | solution.py:196
  228.7 20.9 %collective-permute-start.21 = (bf16[256,1536]{1,0:T(8,128)(2,1)}, bf16[256,1536]{1,0:T(8,128)(2,1)S(1)}, u32[]{:S(2)}, u32[]{:S(2)}) collective-permute-start(bf16[256,1536]{1,0:T(8,128)(2,1)} %get-tuple-element.89), channel_id=1, source_target_pairs={{3,2},{2,1},{7,6},{6,5},{11,10},{10,9},{15,14},{14,13},{19,18},{18... | collective-permute-start | bytes 2359304 | tf_op jit(solution)/shard_map/ppermute | solution.py:196
  237.3 135.8 %reduce-scatter.8.cloned.1.call-start = ((), (), s32[]{:S(2)}) async-start(), calls=%async_computation.6 | async-start | bytes 2654208 | tf_op jit(solution)/shard_map/reduce_scatter | solution.py:877
  238.6 20.1 %collective-permute-start.31 = (bf16[2,1,96,1152]{3,2,1,0:T(8,128)(2,1)S(1)}, bf16[2,1,96,1152]{3,2,1,0:T(8,128)(2,1)S(1)}, u32[]{:S(2)}, u32[]{:S(2)}) collective-permute-start(bf16[2,1,96,1152]{3,2,1,0:T(8,128)(2,1)S(1)} %dynamic-slice_convert_fusion.1), channel_id=1, source_target_pairs={{0,8},{8,0},{16,24},{24,16},{1,9},{9,1},{17,25},{25,17},{2,10},{10... | collective-permute-start | bytes 1327112 | tf_op jit(solution)/shard_map/ppermute | solution.py:26
  251.6 20.4 %collective-permute-start.22 = (bf16[256,1536]{1,0:T(8,128)(2,1)S(1)}, bf16[256,1536]{1,0:T(8,128)(2,1)S(1)}, u32[]{:S(2)}, u32[]{:S(2)}) collective-permute-start(bf16[256,1536]{1,0:T(8,128)(2,1)S(1)} %get-tuple-element.92), channel_id=1, source_target_pairs={{0,1},{1,2},{2,3},{4,5},{5,6},{6,7},{8,9},{9,10},{10,11},{12,13},{... | collective-permute-start | bytes 2359304 | tf_op jit(solution)/shard_map/ppermute | solution.py:196
  253.8 19.9 %collective-permute-start.23 = (bf16[256,1536]{1,0:T(8,128)(2,1)S(1)}, bf16[256,1536]{1,0:T(8,128)(2,1)S(1)}, u32[]{:S(2)}, u32[]{:S(2)}) collective-permute-start(bf16[256,1536]{1,0:T(8,128)(2,1)S(1)} %get-tuple-element.93), channel_id=1, source_target_pairs={{3,2},{2,1},{1,0},{7,6},{6,5},{5,4},{11,10},{10,9},{9,8},{15,14},{... | collective-permute-start | bytes 2359304 | tf_op jit(solution)/shard_map/ppermute | solution.py:196
  258.2 22.4 %collective-permute-start.33 = (bf16[1,2,96,1152]{3,2,1,0:T(8,128)(2,1)S(1)}, bf16[1,2,96,1152]{3,2,1,0:T(8,128)(2,1)S(1)}, u32[]{:S(2)}, u32[]{:S(2)}) collective-permute-start(bf16[1,2,96,1152]{3,2,1,0:T(8,128)(2,1)S(1)} %dynamic-slice_convert_fusion), channel_id=1, source_target_pairs={{0,16},{8,24},{16,0},{24,8},{1,17},{9,25},{17,1},{25,9},{2,18},{10... | collective-permute-start | bytes 1327112 | tf_op jit(solution)/shard_map/ppermute | solution.py:26
  258.8 22.7 %collective-permute-start.32 = (bf16[1,1,96,1152]{3,2,1,0:T(8,128)(2,1)S(1)}, bf16[1,1,96,1152]{3,2,1,0:T(8,128)(2,1)S(1)}, u32[]{:S(2)}, u32[]{:S(2)}) collective-permute-start(bf16[1,1,96,1152]{3,2,1,0:T(8,128)(2,1)S(1)} %dynamic-slice_convert_fusion.3), channel_id=1, source_target_pairs={{0,16},{8,24},{16,0},{24,8},{1,17},{9,25},{17,1},{25,9},{2,18},{10... | collective-permute-start | bytes 663560 | tf_op jit(solution)/shard_map/ppermute | solution.py:26
  274.6 19.2 %collective-permute-start.24 = (bf16[256,1536]{1,0:T(8,128)(2,1)S(1)}, bf16[256,1536]{1,0:T(8,128)(2,1)S(1)}, u32[]{:S(2)}, u32[]{:S(2)}) collective-permute-start(bf16[256,1536]{1,0:T(8,128)(2,1)S(1)} %get-tuple-element.96), channel_id=1, source_target_pairs={{0,1},{1,2},{2,3},{4,5},{5,6},{6,7},{8,9},{9,10},{10,11},{12,13},{... | collective-permute-start | bytes 2359304 | tf_op jit(solution)/shard_map/ppermute | solution.py:196
  276.6 19.1 %collective-permute-start.25 = (bf16[256,1536]{1,0:T(8,128)(2,1)S(1)}, bf16[256,1536]{1,0:T(8,128)(2,1)S(1)}, u32[]{:S(2)}, u32[]{:S(2)}) collective-permute-start(bf16[256,1536]{1,0:T(8,128)(2,1)S(1)} %get-tuple-element.97), channel_id=1, source_target_pairs={{3,2},{2,1},{1,0},{7,6},{6,5},{5,4},{11,10},{10,9},{9,8},{15,14},{... | collective-permute-start | bytes 2359304 | tf_op jit(solution)/shard_map/ppermute | solution.py:196
  281.5 24.9 %collective-permute-start.34 = (bf16[1,1,96,1152]{3,2,1,0:T(8,128)(2,1)}, bf16[1,1,96,1152]{3,2,1,0:T(8,128)(2,1)}, u32[]{:S(2)}, u32[]{:S(2)}) collective-permute-start(bf16[1,1,96,1152]{3,2,1,0:T(8,128)(2,1)} %dynamic-slice_convert_fusion.2), channel_id=1, source_target_pairs={{0,8},{8,0},{16,24},{24,16},{1,9},{9,1},{17,25},{25,17},{2,10},{10... | collective-permute-start | bytes 663560 | tf_op jit(solution)/shard_map/ppermute | solution.py:26
  300.4 18.4 %collective-permute-start.26 = (bf16[256,1536]{1,0:T(8,128)(2,1)S(1)}, bf16[256,1536]{1,0:T(8,128)(2,1)S(1)}, u32[]{:S(2)}, u32[]{:S(2)}) collective-permute-start(bf16[256,1536]{1,0:T(8,128)(2,1)S(1)} %get-tuple-element.100), channel_id=1, source_target_pairs={{1,2},{2,3},{5,6},{6,7},{9,10},{10,11},{13,14},{14,15},{17,18},{18... | collective-permute-start | bytes 2359304 | tf_op jit(solution)/shard_map/ppermute | solution.py:196
  322.9 43.3 %collective-permute-start.28 = (bf16[256,1536]{1,0:T(8,128)(2,1)}, bf16[256,1536]{1,0:T(8,128)(2,1)}, u32[]{:S(2)}, u32[]{:S(2)}) collective-permute-start(bf16[256,1536]{1,0:T(8,128)(2,1)} %get-tuple-element.104), channel_id=1, source_target_pairs={{2,3},{6,7},{10,11},{14,15},{18,19},{22,23},{26,27},{30,31}} | collective-permute-start | bytes 2359304 | tf_op jit(solution)/shard_map/ppermute | solution.py:196
  325.1 41.0 %collective-permute-start.29 = (bf16[256,1536]{1,0:T(8,128)(2,1)}, bf16[256,1536]{1,0:T(8,128)(2,1)}, u32[]{:S(2)}, u32[]{:S(2)}) collective-permute-start(bf16[256,1536]{1,0:T(8,128)(2,1)} %get-tuple-element.105), channel_id=1, source_target_pairs={{1,0},{5,4},{9,8},{13,12},{17,16},{21,20},{25,24},{29,28}} | collective-permute-start | bytes 2359304 | tf_op jit(solution)/shard_map/ppermute | solution.py:196
  343.4 27.3 %collective-permute-start.39 = (f32[208,256]{1,0:T(8,128)S(1)}, f32[208,256]{1,0:T(8,128)S(1)}, u32[]{:S(2)}, u32[]{:S(2)}) collective-permute-start(f32[208,256]{1,0:T(8,128)S(1)} %fusion.23), channel_id=1, source_target_pairs={{0,2},{1,3},{2,0},{3,1},{4,6},{5,7},{6,4},{7,5},{8,10},{9,11},{10,... | collective-permute-start | bytes 638984 | tf_op jit(solution)/shard_map/ppermute | solution.py:26
  (73 other events, 843.3 us)
Sparse Core Ops, SparseCore 0:
  9.9 36.5 all-gather.4
  48.3 28.6 all-gather.2
  141.1 60.6 reduce-scatter.9
  237.4 47.9 reduce-scatter.5
  298.5 41.9 reduce-scatter.7

commit v2 on v1

--- a/solution.py
+++ b/solution.py
@@ -4,6 +4,7 @@
 import jax.numpy as jnp
 from jax import lax
 from jax.experimental import pallas as pl
+from jax.experimental.layout import Layout, with_layout_constraint
 from jax.experimental.pallas import tpu as pltpu
 from jax.sharding import PartitionSpec as P
 
@@ -388,7 +389,7 @@
         functools.partial(forward_outputs_kernel, heads, width),
         grid=(blocks,),
         in_specs=[
-            block(conv), block(3 * LANES), block(width), whole(carry),
+            block(conv), block(2 * LANES), block(width), whole(carry),
             pl.BlockSpec((8, width), lambda b: (b, 0)), block(width), block(width),
             whole(chan), whole(e3),
         ],
@@ -404,7 +405,7 @@
 
 
 def backward_states_kernel(
-    heads, width, total_inner, xbc_ref, dt_ref, y_ref, z_ref, dyn_ref, sums_ref, chan_ref, e3_ref,
+    heads, width, total_inner, read_ref, cum_ref, y_ref, z_ref, dyn_ref, sums_ref, chan_ref, e3_ref,
     yn_ref, dssd_ref, dz_ref, gain_ref, dstate_ref, dfinal_ref, decay_ref,
     dstate, total,
 ):
@@ -416,8 +417,8 @@
         total[...] = jnp.zeros_like(total)
         gain_ref[...] = jnp.zeros_like(gain_ref)
 
-    read = xbc_ref[:, width + LANES : width + 2 * LANES]
-    cum = dt_ref[:, LANES : 2 * LANES]
+    read = read_ref[...]
+    cum = cum_ref[...]
     last = cum[TB - 1 : TB, :]
     grown = split3(head_lanes(jnp.exp(cum), heads))
     row = lax.broadcasted_iota(jnp.int32, (8, LANES), 0)
@@ -455,7 +456,7 @@
 
 
 def backward_states(xbc, dt, y, z, dyn, sums, chan, e3, heads, width, total_inner):
-    rows, conv = xbc.shape
+    rows, _ = xbc.shape
     blocks = rows // TB
     back = blocks - 1
     block = lambda w: pl.BlockSpec((TB, w), lambda i: (back - i, 0))
@@ -464,7 +465,9 @@
         functools.partial(backward_states_kernel, heads, width, float(total_inner)),
         grid=(blocks,),
         in_specs=[
-            block(conv), block(3 * LANES), block(width), block(width), block(width),
+            pl.BlockSpec((TB, LANES), lambda i: (back - i, width // LANES + 1)),
+            pl.BlockSpec((TB, LANES), lambda i: (back - i, 1)),
+            block(width), block(width), block(width),
             pl.BlockSpec((8, TB), lambda i: (0, back - i)), whole(chan), whole(e3),
         ],
         out_specs=[
@@ -840,7 +843,9 @@
     )
     dcarry = shifted_by(dfinal, "col", -1)
 
-    mixed = against(output_full, yn).astype(BF16)
+    mixed = with_layout_constraint(
+        against(output_full, yn).astype(BF16), Layout(major_to_minor=(0, 1))
+    )
     mixed = lax.psum_scatter(mixed, "ta", scatter_dimension=0, tiled=True)
     quarter = mixed.shape[0]
     own = lax.dynamic_slice_in_dim(h, lax.axis_index("ta") * quarter, quarter, 1).astype(F32)

time: 389 us -> 382 us (0.982)
    unnamed x108, local copies, waits for them, and re-layouts: 14.6 us -> 10 us
  transfers between devices with their start and end apart: 45 -> 45, of which waited for: 19 -> 19; matrix products, arithmetic and copies ran while one was open for 25% -> 26% of each run, Pallas kernels for 16% -> 17%
where the time goes in v2:
time: 382 us; the launch traced here: 375 us
  waiting for transfers between devices  96.2 us (25%)
  Pallas kernels  85 us (22%)
  starting transfers between devices  59.7 us (16%)
  matrix products  56.3 us (15%)
  other arithmetic  34.9 us (9%)
  local copies, waits for them, and re-layouts  27.3 us (7%)
  between operations  15.7 us (4%)
    ppermute x12, waiting for transfers between devices, chain_sum_step(): out = [lax.ppermute(sends[side], axis, pairs[side]) for side in range(2)]  60.2 us
    ppermute x24, waiting for transfers between devices, swap_bit(): return lax.ppermute(value, axis, bit_pairs(axis, bit))  34.7 us
    ppermute x12, starting transfers between devices, chain_sum_step(): out = [lax.ppermute(sends[side], axis, pairs[side]) for side in range(2)]  30.3 us
    pallas_call x1, Pallas kernels, backward_inputs(): pl.pallas_call(functools.partial(backward_inputs_kernel, heads, width, st...  26.5 us
    dot_general x4, matrix products, product(): return jnp.dot(left, right, preferred_element_type=F32)  22.3 us
    ppermute x24, starting transfers between devices, swap_bit(): return lax.ppermute(value, axis, bit_pairs(axis, bit))  21.7 us
    pallas_call x4, Pallas kernels, finish(): pl.pallas_call(functools.partial(finish_kernel, 'ta', count, steps, so_fa...  18 us
    dot_general x3, matrix products, against(): lax.dot_general(left, right, (((1,), (1,)), ((), ())), preferred_element_...  17.3 us
  transfers between devices with their start and end apart: 45, of which 19 were waited for; matrix products, arithmetic and copies ran while one was open for 26% of the time, Pallas kernels for 17%

profile of v2, /device:TPU:18, one launch (start us, length us, event | category | flops | bytes accessed | tf_op | source)
XLA Modules:
  0.0 375.2 jit_solution(12211951276497426525)
XLA Ops:
  35.3 9.7 %collective-permute-done.5.refs_3_ = bf16[96,1152]{1,0:T(8,128)(2,1)S(1)} collective-permute-done((bf16[96,1152]{1,0:T(8,128)(2,1)S(1)}, bf16[96,1152]{1,0:T(8,128)(2,1)S(1)}, u32[]{:S(2)}, u32[]{:S(2)}) %collective-permute-start.5) | collective-permute-done | bytes 221216 | tf_op jit(solution)/shard_map/ppermute | solution.py:27
  55.9 5.8 %fusion.26.pre_ref = f32[1024,1152]{1,0:T(8,128)} fusion(bf16[1024,1536]{1,0:T(8,128)(2,1)S(1)} %fusion.2, bf16[1536,1152]{1,0:T(8,128)(2,1)S(1)} %bitcast.94), kind=kOutput, calls=%fused_computation.103 | convolution fusion | flops 3623878656 | bytes 11403264 | tf_op jit(solution)/shard_map/dot_general | solution.py:761
  61.7 13.6 %forward_states.1 = (bf16[1024,1024]{1,0:T(8,128)(2,1)}, bf16[1024,1024]{1,0:T(8,128)(2,1)}, bf16[1024,1024]{1,0:T(8,128)(2,1)}, f32[1024,384]{1,0:T(8,128)}, f3...) custom-call(f32[1024,1152]{1,0:T(8,128)} %fusion.26.pre_ref, f32[8,1152]{1,0:T(8,128)S(1)} %fusion.27.halo_ref, ...), custom_call_target="tpu_custom_call" | custom-call | tf_op jit(solution)/shard_map/forward_states/pallas_call | solution.py:313
  77.8 6.9 %fusion.7.dyn_ref = f32[1024,768]{1,0:T(8,128)} fusion(bf16[1536,768]{1,0:T(8,128)(2,1)} %all-gather.5.cloned.1.call-done, f32[1024]{0:T(1024)S(1)} %fusion.18, bf16[1,1024,1536]{2,1,0:T(8,128)(2,1)} %param.33), kind=kOutput, calls=%fused_computation.28 | convolution fusion | flops 2420637696 | bytes 8654848 | tf_op jit(solution)/shard_map/dot_general | solution.py:761
  84.7 6.9 %fusion.28.z_ref = f32[1024,768]{1,0:T(8,128)} fusion(bf16[1024,1536]{1,0:T(8,128)(2,1)} %copy-done.21, bf16[1536,768]{1,0:T(8,128)(2,1)} %all-gather.3.cloned.1.call-done), kind=kOutput, calls=%fused_computation.105 | convolution fusion | flops 2415919104 | bytes 8650752 | tf_op jit(solution)/shard_map/dot_general | solution.py:761
  91.6 11.8 %forward_outputs.1 = (f32[1024,768]{1,0:T(8,128)}, bf16[1024,768]{1,0:T(8,128)(2,1)}, f32[8,1024]{1,0:T(8,128)S(1)}) custom-call(bf16[1024,1024]{1,0:T(8,128)(2,1)} %get-tuple-element.65.xbc_ref.read_ref, f32[1024,384]{1,0:T(8,128)} %get-tuple-element.66.dt_ref.cum_ref, f32[1024,768]{1,0:T(8,128)} %get-tuple-element.67.state_ref, ...), custom_call_target="tpu_custom_call" | custom-call | tf_op jit(solution)/shard_map/forward_outputs/pallas_call | solution.py:388
  112.2 10.9 %backward_states.1 = (bf16[1024,768]{1,0:T(8,128)(2,1)}, bf16[1024,768]{1,0:T(8,128)(2,1)}, bf16[1024,768]{1,0:T(8,128)(2,1)}, f32[8,768]{1,0:T(8,128)S(1)}, f32...) custom-call(bf16[1024,1024]{1,0:T(8,128)(2,1)} %get-tuple-element.65.xbc_ref.read_ref, ...), custom_call_target="tpu_custom_call" | custom-call | tf_op jit(solution)/shard_map/backward_states/pallas_call | solution.py:464
  123.1 5.7 %convolution_convert_fusion.2 = bf16[1536,768]{1,0:T(8,128)(2,1)} fusion(bf16[1024,768]{1,0:T(8,128)(2,1)} %get-tuple-element.72, f32[1024]{0:T(1024)S(1)} %fusion.18, bf16[1,1024,1536]{2,1,0:T(8,128)(2,1)S(1)} %copy-done.8), kind=kOutput, calls=%fused_computation.10 | convolution fusion | flops 2421817344 | bytes 7081984 | tf_op jit(solution)/shard_map/dot_general | solution.py:753
  128.7 6.5 %fusion.3 = bf16[1536,1024]{1,0:T(8,128)(2,1)} fusion(bf16[1024,768]{1,0:T(8,128)(2,1)} %get-tuple-element.72, bf16[1536,768]{1,0:T(8,128)(2,1)} %all-gather.5.cloned.1.call-done), kind=kOutput, calls=%fused_computation.12 | convolution fusion | flops 2417491968 | bytes 7077888 | tf_op jit(solution)/shard_map/dot_general | solution.py:757
  137.0 6.2 %fusion.29 = f32[1024,1536]{1,0:T(8,128)} fusion(bf16[1024,768]{1,0:T(8,128)(2,1)S(1)} %copy-done.48, bf16[1536,768]{1,0:T(8,128)(2,1)} %all-gather.3.cloned.1.call-done), kind=kOutput, calls=%fused_computation.106 | convolution fusion | flops 2415919104 | bytes 10223616 | tf_op jit(solution)/shard_map/dot_general | solution.py:757
  143.2 26.5 %backward_inputs.1 = (bf16[1024,1152]{1,0:T(8,128)(2,1)}, f32[8,1024]{1,0:T(8,128)S(1)}, f32[8,1024]{1,0:T(8,128)}, f32[8,1024]{1,0:T(8,128)S(1)}, f32[40,1024]{...) custom-call(bf16[1024,1024]{1,0:T(8,128)(2,1)} %get-tuple-element.65.xbc_ref.read_ref, ...), custom_call_target="tpu_custom_call" | custom-call | tf_op jit(solution)/shard_map/backward_inputs/pallas_call | solution.py:633
  173.5 7.0 %convolution_convert_fusion = bf16[1536,1152]{1,0:T(8,128)(2,1)S(1)} fusion(bf16[1024,1536]{1,0:T(8,128)(2,1)} %copy-done.21, bf16[1024,1152]{1,0:T(8,128)(2,1)} %fusion.15), kind=kOutput, calls=%fused_computation.2 | convolution fusion | flops 3625648128 | bytes 9043968 | tf_op jit(solution)/shard_map/dot_general | solution.py:753
  184.5 4.5 %add_convert_fusion.own_ref = bf16[1024,1536]{1,0:T(8,128)(2,1)S(1)} fusion(f32[1024,1536]{1,0:T(8,128)S(1)} %copy-done.51, bf16[1024,1152]{1,0:T(8,128)(2,1)S(1)} %copy-done.47, bf16[1536,1152]{1,0:T(8,128)(2,1)S(1)} %bitcast.95), kind=kOutput, calls=%fused_computation.6 | convolution fusion | flops 3627024384 | bytes 15335424 | tf_op jit(solution)/shard_map/dot_general | solution.py:757
  202.2 11.9 %collective-permute-done.19.rest_3_ = bf16[256,1536]{1,0:T(8,128)(2,1)S(1)} collective-permute-done((bf16[256,1536]{1,0:T(8,128)(2,1)}, bf16[256,1536]{1,0:T(8,128)(2,1)S(1)}, u32[]{:S(2)}, u32[]{:S(2)}) %collective-permute-start.19) | collective-permute-done | bytes 786464 | tf_op jit(solution)/shard_map/ppermute | solution.py:197
  220.8 4.5 %collective-permute-start.21 = (bf16[256,1536]{1,0:T(8,128)(2,1)}, bf16[256,1536]{1,0:T(8,128)(2,1)S(1)}, u32[]{:S(2)}, u32[]{:S(2)}) collective-permute-start(bf16[256,1536]{1,0:T(8,128)(2,1)} %get-tuple-element.89), channel_id=1, source_target_pairs={{3,2},{2,1},{7,6},{6,5},{11,10},{10,9},{15,14},{14,13},{19,18},{18... | collective-permute-start | bytes 2359304 | tf_op jit(solution)/shard_map/ppermute | solution.py:197
  231.3 9.0 %collective-permute-done.20.rest_1_.rest_0_ = bf16[256,1536]{1,0:T(8,128)(2,1)S(1)} collective-permute-done((bf16[256,1536]{1,0:T(8,128)(2,1)}, bf16[256,1536]{1,0:T(8,128)(2,1)S(1)}, u32[]{:S(2)}, u32[]{:S(2)}) %collective-permute-start.20) | collective-permute-done | bytes 786464 | tf_op jit(solution)/shard_map/ppermute | solution.py:197
  252.6 11.6 %collective-permute-done.22.rest_2_.rest_1_.rest_0_ = bf16[256,1536]{1,0:T(8,128)(2,1)S(1)} collective-permute-done((bf16[256,1536]{1,0:T(8,128)(2,1)S(1)}, bf16[256,1536]{1,0:T(8,128)(2,1)S(1)}, u32[]{:S(2)}, u32[]{:S(2)}) %collective-permute-start.22) | collective-permute-done | bytes 786464 | tf_op jit(solution)/shard_map/ppermute | solution.py:197
  274.5 11.4 %collective-permute-done.24.rest_2_.rest_1_.rest_0_ = bf16[256,1536]{1,0:T(8,128)(2,1)S(1)} collective-permute-done((bf16[256,1536]{1,0:T(8,128)(2,1)S(1)}, bf16[256,1536]{1,0:T(8,128)(2,1)S(1)}, u32[]{:S(2)}, u32[]{:S(2)}) %collective-permute-start.24) | collective-permute-done | bytes 786464 | tf_op jit(solution)/shard_map/ppermute | solution.py:197
  300.2 10.1 %collective-permute-done.26.rest_2_.rest_1_ = bf16[256,1536]{1,0:T(8,128)(2,1)S(1)} collective-permute-done((bf16[256,1536]{1,0:T(8,128)(2,1)S(1)}, bf16[256,1536]{1,0:T(8,128)(2,1)S(1)}, u32[]{:S(2)}, u32[]{:S(2)}) %collective-permute-start.26) | collective-permute-done | bytes 786464 | tf_op jit(solution)/shard_map/ppermute | solution.py:197
  320.9 13.0 %collective-permute-done.38 = f32[208,256]{1,0:T(8,128)} collective-permute-done((f32[208,256]{1,0:T(8,128)}, f32[208,256]{1,0:T(8,128)}, u32[]{:S(2)}, u32[]{:S(2)}) %collective-permute-start.38) | collective-permute-done | bytes 213024 | tf_op jit(solution)/shard_map/ppermute | solution.py:27
  335.0 6.6 %collective-permute-start.39 = (f32[208,256]{1,0:T(8,128)S(1)}, f32[208,256]{1,0:T(8,128)}, u32[]{:S(2)}, u32[]{:S(2)}) collective-permute-start(f32[208,256]{1,0:T(8,128)S(1)} %fusion.23), channel_id=1, source_target_pairs={{0,2},{1,3},{2,0},{3,1},{4,6},{5,7},{6,4},{7,5},{8,10},{9,11},{10,... | collective-permute-start | bytes 638984 | tf_op jit(solution)/shard_map/ppermute | solution.py:27
  345.1 4.5 %finish.4.rest_6_ = f32[1024,1536]{1,0:T(8,128)} custom-call(bf16[1024,1536]{1,0:T(8,128)(2,1)} %copy-done.6, bf16[1024,1536]{1,0:T(8,128)(2,1)} %bitcast.84, bf16[1024,1536]{1,0:T(8,128)(2,1)} %bitcast.89, f32[8,1536]{1,0:T(8,128)S(1)} %mul.118.gain_ref, bf16[256,1536]{1,0:T(8,128)(2,1)S(1)} %collective-permute-done.18.rest_0_, ...), custom_call_target="tpu_custom_call" | custom-call | tf_op jit(solution)/shard_map/finish/pallas_call | solution.py:739
  349.6 4.5 %finish.5.rest_6_ = f32[1024,1536]{1,0:T(8,128)} custom-call(bf16[1024,1536]{1,0:T(8,128)(2,1)} %copy-done.6, bf16[1024,1536]{1,0:T(8,128)(2,1)} %bitcast.85, bf16[1024,1536]{1,0:T(8,128)(2,1)} %bitcast.90, f32[8,1536]{1,0:T(8,128)S(1)} %mul.118.gain_ref, ...), custom_call_target="tpu_custom_call", output_to_operand_aliasing={{}: (10, {})} | custom-call | tf_op jit(solution)/shard_map/finish/pallas_call | solution.py:739
  354.2 4.5 %finish.6.rest_6_ = f32[1024,1536]{1,0:T(8,128)} custom-call(bf16[1024,1536]{1,0:T(8,128)(2,1)} %copy-done.6, bf16[1024,1536]{1,0:T(8,128)(2,1)} %bitcast.86, bf16[1024,1536]{1,0:T(8,128)(2,1)} %bitcast.91, f32[8,1536]{1,0:T(8,128)S(1)} %mul.118.gain_ref, bf16[256,1536]{1,0:T(8,128)(2,1)S(1)} %copy-done.1, ...), custom_call_target="tpu_custom_call", output_to_operand_aliasing={{}: (10, {})} | custom-call | tf_op jit(solution)/shard_map/finish/pallas_call | solution.py:739
  (299 shorter events, 145.7 us)
Async XLA Ops:
  7.2 70.6 %all-gather.5.cloned.1.call-start = ((), (), s32[]{:S(2)}) async-start(), calls=%async_computation.4 | async-start | bytes 2654208 | tf_op jit(solution)/shard_map/all_gather | solution.py:793
  8.0 76.7 %all-gather.3.cloned.1.call-start = ((), (), s32[]{:S(2)}) async-start(), calls=%async_computation.3 | async-start | bytes 2654208 | tf_op jit(solution)/shard_map/all_gather | solution.py:792
  10.0 23.0 %collective-permute-start.3 = (bf16[192,1152]{1,0:T(8,128)(2,1)S(1)}, bf16[192,1152]{1,0:T(8,128)(2,1)S(1)}, u32[]{:S(2)}, u32[]{:S(2)}) collective-permute-start(bf16[192,1152]{1,0:T(8,128)(2,1)S(1)} %concatenate.30.refs_0_), channel_id=1, source_target_pairs={{0,8},{8,0},{16,24},{24,16},{1,9},{9,1},{17,25},{25,17},{2,10},{10... | collective-permute-start | bytes 1327112 | tf_op jit(solution)/shard_map/ppermute | solution.py:27
  10.6 24.0 %collective-permute-start.4 = (bf16[192,1152]{1,0:T(8,128)(2,1)S(1)}, bf16[192,1152]{1,0:T(8,128)(2,1)S(1)}, u32[]{:S(2)}, u32[]{:S(2)}) collective-permute-start(bf16[192,1152]{1,0:T(8,128)(2,1)S(1)} %concatenate.30.refs_0_), channel_id=1, source_target_pairs={{0,16},{8,24},{16,0},{24,8},{1,17},{9,25},{17,1},{25,9},{2,18},{10... | collective-permute-start | bytes 1327112 | tf_op jit(solution)/shard_map/ppermute | solution.py:27
  12.1 33.5 %collective-permute-start.7 = (bf16[192,1152]{1,0:T(8,128)(2,1)S(1)}, bf16[192,1152]{1,0:T(8,128)(2,1)S(1)}, u32[]{:S(2)}, u32[]{:S(2)}) collective-permute-start(bf16[192,1152]{1,0:T(8,128)(2,1)S(1)} %concatenate.30.refs_0_), channel_id=1, source_target_pairs={{0,4},{4,0},{1,5},{5,1},{2,6},{6,2},{3,7},{7,3},{8,12},{12,8},{9,1... | collective-permute-start | bytes 1327112 | tf_op jit(solution)/shard_map/ppermute | solution.py:27
  17.3 202.2 %reduce-scatter.4.cloned.1.call-start = ((), (), s32[]{:S(2)}) async-start(), calls=%async_computation.5 | async-start | bytes 3932160 | tf_op jit(solution)/shard_map/reduce_scatter | solution.py:849
  135.3 152.6 %reduce-scatter.6.cloned.1.call-start = ((), (), s32[]{:S(2)}) async-start(), calls=%async_computation.6 | async-start | bytes 2654208 | tf_op jit(solution)/shard_map/reduce_scatter | solution.py:882
  182.0 35.3 %collective-permute-start.30 = (bf16[4,192,1152]{2,1,0:T(8,128)(2,1)}, bf16[4,192,1152]{2,1,0:T(8,128)(2,1)S(1)}, u32[]{:S(2)}, u32[]{:S(2)}) collective-permute-start(bf16[4,192,1152]{2,1,0:T(8,128)(2,1)} %dynamic-slice_bitcast_fusion), channel_id=1, source_target_pairs={{0,4},{4,0},{1,5},{5,1},{2,6},{6,2},{3,7},{7,3},{8,12},{12,8},{9,1... | collective-permute-start | bytes 5308424 | tf_op jit(solution)/shard_map/ppermute | solution.py:27
  192.4 21.7 %collective-permute-start.19 = (bf16[256,1536]{1,0:T(8,128)(2,1)}, bf16[256,1536]{1,0:T(8,128)(2,1)S(1)}, u32[]{:S(2)}, u32[]{:S(2)}) collective-permute-start(bf16[256,1536]{1,0:T(8,128)(2,1)} %dynamic_slice.87), channel_id=1, source_target_pairs={{3,2},{7,6},{11,10},{15,14},{19,18},{23,22},{27,26},{31,30}} | collective-permute-start | bytes 2359304 | tf_op jit(solution)/shard_map/ppermute | solution.py:197
  219.5 20.9 %collective-permute-start.20 = (bf16[256,1536]{1,0:T(8,128)(2,1)}, bf16[256,1536]{1,0:T(8,128)(2,1)S(1)}, u32[]{:S(2)}, u32[]{:S(2)}) collective-permute-start(bf16[256,1536]{1,0:T(8,128)(2,1)} %get-tuple-element.88), channel_id=1, source_target_pairs={{0,1},{1,2},{4,5},{5,6},{8,9},{9,10},{12,13},{13,14},{16,17},{17,1... | collective-permute-start | bytes 2359304 | tf_op jit(solution)/shard_map/ppermute | solution.py:197
  220.8 20.9 %collective-permute-start.21 = (bf16[256,1536]{1,0:T(8,128)(2,1)}, bf16[256,1536]{1,0:T(8,128)(2,1)S(1)}, u32[]{:S(2)}, u32[]{:S(2)}) collective-permute-start(bf16[256,1536]{1,0:T(8,128)(2,1)} %get-tuple-element.89), channel_id=1, source_target_pairs={{3,2},{2,1},{7,6},{6,5},{11,10},{10,9},{15,14},{14,13},{19,18},{18... | collective-permute-start | bytes 2359304 | tf_op jit(solution)/shard_map/ppermute | solution.py:197
  229.4 137.2 %reduce-scatter.8.cloned.1.call-start = ((), (), s32[]{:S(2)}) async-start(), calls=%async_computation.7 | async-start | bytes 2654208 | tf_op jit(solution)/shard_map/reduce_scatter | solution.py:882
  230.7 20.1 %collective-permute-start.31 = (bf16[2,1,96,1152]{3,2,1,0:T(8,128)(2,1)S(1)}, bf16[2,1,96,1152]{3,2,1,0:T(8,128)(2,1)S(1)}, u32[]{:S(2)}, u32[]{:S(2)}) collective-permute-start(bf16[2,1,96,1152]{3,2,1,0:T(8,128)(2,1)S(1)} %dynamic-slice_convert_fusion.1), channel_id=1, source_target_pairs={{0,8},{8,0},{16,24},{24,16},{1,9},{9,1},{17,25},{25,17},{2,10},{10... | collective-permute-start | bytes 1327112 | tf_op jit(solution)/shard_map/ppermute | solution.py:27
  243.7 20.4 %collective-permute-start.22 = (bf16[256,1536]{1,0:T(8,128)(2,1)S(1)}, bf16[256,1536]{1,0:T(8,128)(2,1)S(1)}, u32[]{:S(2)}, u32[]{:S(2)}) collective-permute-start(bf16[256,1536]{1,0:T(8,128)(2,1)S(1)} %get-tuple-element.92), channel_id=1, source_target_pairs={{0,1},{1,2},{2,3},{4,5},{5,6},{6,7},{8,9},{9,10},{10,11},{12,13},{... | collective-permute-start | bytes 2359304 | tf_op jit(solution)/shard_map/ppermute | solution.py:197
  245.9 19.9 %collective-permute-start.23 = (bf16[256,1536]{1,0:T(8,128)(2,1)S(1)}, bf16[256,1536]{1,0:T(8,128)(2,1)S(1)}, u32[]{:S(2)}, u32[]{:S(2)}) collective-permute-start(bf16[256,1536]{1,0:T(8,128)(2,1)S(1)} %get-tuple-element.93), channel_id=1, source_target_pairs={{3,2},{2,1},{1,0},{7,6},{6,5},{5,4},{11,10},{10,9},{9,8},{15,14},{... | collective-permute-start | bytes 2359304 | tf_op jit(solution)/shard_map/ppermute | solution.py:197
  250.3 22.5 %collective-permute-start.33 = (bf16[1,2,96,1152]{3,2,1,0:T(8,128)(2,1)S(1)}, bf16[1,2,96,1152]{3,2,1,0:T(8,128)(2,1)S(1)}, u32[]{:S(2)}, u32[]{:S(2)}) collective-permute-start(bf16[1,2,96,1152]{3,2,1,0:T(8,128)(2,1)S(1)} %dynamic-slice_convert_fusion), channel_id=1, source_target_pairs={{0,16},{8,24},{16,0},{24,8},{1,17},{9,25},{17,1},{25,9},{2,18},{10... | collective-permute-start | bytes 1327112 | tf_op jit(solution)/shard_map/ppermute | solution.py:27
  250.9 22.7 %collective-permute-start.32 = (bf16[1,1,96,1152]{3,2,1,0:T(8,128)(2,1)S(1)}, bf16[1,1,96,1152]{3,2,1,0:T(8,128)(2,1)S(1)}, u32[]{:S(2)}, u32[]{:S(2)}) collective-permute-start(bf16[1,1,96,1152]{3,2,1,0:T(8,128)(2,1)S(1)} %dynamic-slice_convert_fusion.3), channel_id=1, source_target_pairs={{0,16},{8,24},{16,0},{24,8},{1,17},{9,25},{17,1},{25,9},{2,18},{10... | collective-permute-start | bytes 663560 | tf_op jit(solution)/shard_map/ppermute | solution.py:27
  266.7 19.2 %collective-permute-start.24 = (bf16[256,1536]{1,0:T(8,128)(2,1)S(1)}, bf16[256,1536]{1,0:T(8,128)(2,1)S(1)}, u32[]{:S(2)}, u32[]{:S(2)}) collective-permute-start(bf16[256,1536]{1,0:T(8,128)(2,1)S(1)} %get-tuple-element.96), channel_id=1, source_target_pairs={{0,1},{1,2},{2,3},{4,5},{5,6},{6,7},{8,9},{9,10},{10,11},{12,13},{... | collective-permute-start | bytes 2359304 | tf_op jit(solution)/shard_map/ppermute | solution.py:197
  268.8 19.1 %collective-permute-start.25 = (bf16[256,1536]{1,0:T(8,128)(2,1)S(1)}, bf16[256,1536]{1,0:T(8,128)(2,1)S(1)}, u32[]{:S(2)}, u32[]{:S(2)}) collective-permute-start(bf16[256,1536]{1,0:T(8,128)(2,1)S(1)} %get-tuple-element.97), channel_id=1, source_target_pairs={{3,2},{2,1},{1,0},{7,6},{6,5},{5,4},{11,10},{10,9},{9,8},{15,14},{... | collective-permute-start | bytes 2359304 | tf_op jit(solution)/shard_map/ppermute | solution.py:197
  273.6 24.3 %collective-permute-start.34 = (bf16[1,1,96,1152]{3,2,1,0:T(8,128)(2,1)}, bf16[1,1,96,1152]{3,2,1,0:T(8,128)(2,1)}, u32[]{:S(2)}, u32[]{:S(2)}) collective-permute-start(bf16[1,1,96,1152]{3,2,1,0:T(8,128)(2,1)} %dynamic-slice_convert_fusion.2), channel_id=1, source_target_pairs={{0,8},{8,0},{16,24},{24,16},{1,9},{9,1},{17,25},{25,17},{2,10},{10... | collective-permute-start | bytes 663560 | tf_op jit(solution)/shard_map/ppermute | solution.py:27
  291.9 18.4 %collective-permute-start.26 = (bf16[256,1536]{1,0:T(8,128)(2,1)S(1)}, bf16[256,1536]{1,0:T(8,128)(2,1)S(1)}, u32[]{:S(2)}, u32[]{:S(2)}) collective-permute-start(bf16[256,1536]{1,0:T(8,128)(2,1)S(1)} %get-tuple-element.100), channel_id=1, source_target_pairs={{1,2},{2,3},{5,6},{6,7},{9,10},{10,11},{13,14},{14,15},{17,18},{18... | collective-permute-start | bytes 2359304 | tf_op jit(solution)/shard_map/ppermute | solution.py:197
  314.5 44.2 %collective-permute-start.28 = (bf16[256,1536]{1,0:T(8,128)(2,1)}, bf16[256,1536]{1,0:T(8,128)(2,1)}, u32[]{:S(2)}, u32[]{:S(2)}) collective-permute-start(bf16[256,1536]{1,0:T(8,128)(2,1)} %get-tuple-element.104), channel_id=1, source_target_pairs={{2,3},{6,7},{10,11},{14,15},{18,19},{22,23},{26,27},{30,31}} | collective-permute-start | bytes 2359304 | tf_op jit(solution)/shard_map/ppermute | solution.py:197
  316.7 42.0 %collective-permute-start.29 = (bf16[256,1536]{1,0:T(8,128)(2,1)}, bf16[256,1536]{1,0:T(8,128)(2,1)}, u32[]{:S(2)}, u32[]{:S(2)}) collective-permute-start(bf16[256,1536]{1,0:T(8,128)(2,1)} %get-tuple-element.105), channel_id=1, source_target_pairs={{1,0},{5,4},{9,8},{13,12},{17,16},{21,20},{25,24},{29,28}} | collective-permute-start | bytes 2359304 | tf_op jit(solution)/shard_map/ppermute | solution.py:197
  335.0 28.2 %collective-permute-start.39 = (f32[208,256]{1,0:T(8,128)S(1)}, f32[208,256]{1,0:T(8,128)}, u32[]{:S(2)}, u32[]{:S(2)}) collective-permute-start(f32[208,256]{1,0:T(8,128)S(1)} %fusion.23), channel_id=1, source_target_pairs={{0,2},{1,3},{2,0},{3,1},{4,6},{5,7},{6,4},{7,5},{8,10},{9,11},{10,... | collective-permute-start | bytes 638984 | tf_op jit(solution)/shard_map/ppermute | solution.py:27
  (73 other events, 1103.3 us)
Sparse Core Ops, SparseCore 0:
  9.9 36.5 all-gather.4
  48.3 28.6 all-gather.2
  135.4 60.6 reduce-scatter.3
  229.5 47.9 reduce-scatter.5
  290.1 41.9 reduce-scatter.7
